TPU v7x, 32 devices: a whole 2x2x4 slice. The times are simulated.
32 devices in a mesh: wide: 16 (over z, y, x), narrow: 2 (over core).
Axes of the slice: x: 2, y: 2, z: 4, core: 2. Of those that a mesh axis runs over, the one named last changes fastest.
Arguments:
- tokens: bfloat16 [64, 1024, 576], P('wide', 'narrow'), may hold values from -6 to 6
- cotangent: bfloat16 [64, 1024, 576], P('wide', 'narrow'), may hold values from -6 to 6
- documents: int32 [64, 1024], P('wide'), may hold values from 0 to 2, as said below
- attention_master: float32 [1536, 576], P(('wide', 'narrow'))
- attention_first: float32 [1536, 576], P(('wide', 'narrow')), may hold values from -0.00036621094 to 0.00036621094
- attention_second: float32 [1536, 576], P(('wide', 'narrow')), may hold values from 2.2605614e-11 to 3.673412e-10
- feedforward_master: float32 [3, 1536, 576], P(None, ('narrow', 'wide'))
- feedforward_first: float32 [3, 1536, 576], P(None, ('narrow', 'wide')), may hold values from -0.0008544922 to 0.0008544922
- feedforward_second: float32 [3, 1536, 576], P(None, ('narrow', 'wide')), may hold values from 1.4128508e-10 to 2.2605613e-09
- gain_master: float32 [2, 576], replicated, may hold values from 0.5 to 1.5
- gain_first: float32 [2, 576], replicated, may hold values from -0.0034179688 to 0.0034179688
- gain_second: float32 [2, 576], replicated, may hold values from 2.2605613e-09 to 3.616898e-08
Outputs:
- outputs: bfloat16 [64, 1024, 576], P('wide', 'narrow')
- grad_tokens: float32 [64, 1024, 576], P('wide', 'narrow')
- grad_norm: float32 [], replicated
- attention_new: float32 [1536, 576], P(('wide', 'narrow'))
- attention_first_new: float32 [1536, 576], P(('wide', 'narrow'))
- attention_second_new: float32 [1536, 576], P(('wide', 'narrow'))
- feedforward_new: float32 [3, 1536, 576], P(None, ('narrow', 'wide'))
- feedforward_first_new: float32 [3, 1536, 576], P(None, ('narrow', 'wide'))
- feedforward_second_new: float32 [3, 1536, 576], P(None, ('narrow', 'wide'))
- gain_new: float32 [2, 576], replicated
- gain_first_new: float32 [2, 576], replicated
- gain_second_new: float32 [2, 576], replicated
Inputs may be any that keep to these rules, and one draw needn't show every extreme that they name: Each row holds three documents in order (numbers 0, 1, 2, never falling); document 1 starts at position 256 or earlier and runs through position 767 at least.
All inputs are finite; a program needn't handle non-finite values.
Results may differ from a plain program's by a relative error of at most 0.015.
Values may be sent and summed in bfloat16 or wider, within the bound.
No kernel may reach another device: no remote copies, remote signals or barrier semaphores. Data moves between devices by JAX's collectives and lax.ppermute only.
A program may use at most 192 MiB of HBM per device.

v0:
```python
import jax
import jax.numpy as jnp
from jax import lax
from jax.sharding import PartitionSpec as P

D = 576
HEADS = 9
KV_HEADS = 3
HEAD_DIM = 64
STEP = 10
KV_WIDTH = 192


norm_epsilon = 1e-05
adam_epsilon = 1e-08
beta_first = 0.9
beta_second = 0.999
weight_decay = 0.1
rate_matrix = 0.05
rate_gain = 0.5
clip_limit = 1.0
rotary_base = 10000.0
masked_value = -1e30


def rotary_tables(positions, head_width):
    halves = head_width // 2
    frequency = rotary_base ** (-2.0 * jnp.arange(halves, dtype=jnp.float32) / head_width)
    angles = positions.astype(jnp.float32)[:, None] * frequency[None, :]
    return (jnp.cos(angles)[:, None, :], jnp.sin(angles)[:, None, :])


def rotate(values, cosine_table, sine_table):
    halves = values.shape[-1] // 2
    front_part = values[..., :halves]
    behind = values[..., halves:]
    return jnp.concatenate(
        [
            front_part * cosine_table - behind * sine_table,
            behind * cosine_table + front_part * sine_table,
        ],
        axis=-1,
    )


def rotate_back(incoming, cosine_table, sine_table):
    halves = incoming.shape[-1] // 2
    front_part = incoming[..., :halves]
    behind = incoming[..., halves:]
    return jnp.concatenate(
        [
            front_part * cosine_table + behind * sine_table,
            behind * cosine_table - front_part * sine_table,
        ],
        axis=-1,
    )


def adamw_update(master, first_state, second_state, gradient, factor, step_rate, decay_rate):
    clipped = gradient * factor
    first_new = beta_first * first_state + (1.0 - beta_first) * clipped
    second_new = beta_second * second_state + (1.0 - beta_second) * clipped * clipped
    first_hat = first_new / (1.0 - beta_first**STEP)
    second_hat = second_new / (1.0 - beta_second**STEP)
    master_new = master * (1.0 - step_rate * decay_rate) - step_rate * first_hat / (
        jnp.sqrt(second_hat) + adam_epsilon
    )
    return (master_new, first_new, second_new)


def per_device(
    tokens,
    cotangent,
    documents,
    attention_master,
    attention_first,
    attention_second,
    feedforward_master,
    feedforward_first,
    feedforward_second,
    gain_master,
    gain_first,
    gain_second,
):
    seq_count, half_len, model_width = tokens.shape
    narrow_count = lax.axis_size("narrow")
    narrow_place = lax.axis_index("narrow")
    full_len = half_len * narrow_count
    qkv_width = D + 2 * KV_WIDTH
    head_ratio = HEADS // KV_HEADS
    group_size = min(seq_count, max(1, 512 // half_len))
    block_count = seq_count // group_size
    attention_low = lax.all_gather(
        attention_master.astype(jnp.bfloat16), ("wide", "narrow"), axis=0, tiled=True
    )
    feedforward_half = lax.all_gather(
        feedforward_master.astype(jnp.bfloat16), "wide", axis=1, tiled=True
    )
    qkv_rows = attention_low[:qkv_width]
    out_rows = attention_low[qkv_width:]
    residual_first = tokens.astype(jnp.float32)
    inv_first = lax.rsqrt(
        jnp.mean(residual_first * residual_first, axis=-1, keepdims=True) + norm_epsilon
    )
    normal_first = residual_first * inv_first
    normed_first = (normal_first * gain_master[0]).astype(jnp.bfloat16)
    projected = jnp.einsum(
        "spd,jd->spj", normed_first, qkv_rows, preferred_element_type=jnp.float32
    )
    offset = narrow_place * half_len
    query_place = offset + jnp.arange(half_len, dtype=jnp.int32)
    key_place = jnp.arange(full_len, dtype=jnp.int32)
    cosine_table, sine_table = rotary_tables(query_place, HEAD_DIM)
    query_heads = projected[..., :D].reshape(seq_count, half_len, HEADS, HEAD_DIM)
    queries = (rotate(query_heads, cosine_table, sine_table) * HEAD_DIM ** (-0.5)).astype(
        jnp.bfloat16
    )
    key_heads = projected[..., D : D + KV_WIDTH].reshape(seq_count, half_len, KV_HEADS, HEAD_DIM)
    own_keys = rotate(key_heads, cosine_table, sine_table).astype(jnp.bfloat16)
    own_values = (
        projected[..., D + KV_WIDTH :]
        .reshape(seq_count, half_len, KV_HEADS, HEAD_DIM)
        .astype(jnp.bfloat16)
    )
    key_all, value_all = (
        lax.all_gather(own_keys, "narrow", axis=1, tiled=True),
        lax.all_gather(own_values, "narrow", axis=1, tiled=True),
    )
    query_docs = lax.dynamic_slice_in_dim(documents, offset, half_len, 1)
    allowed_place = key_place[None, :] <= query_place[:, None]

    def blocks(tensor):
        return tensor.reshape((block_count, group_size) + tensor.shape[1:])

    def unblock(tensor):
        return tensor.reshape((seq_count,) + tensor.shape[2:])

    def visible(query_doc_part, key_doc_part):
        return (allowed_place[None] & (query_doc_part[:, :, None] == key_doc_part[:, None, :]))[
            :, None, None
        ]

    def attend(members):
        query_part, key_part, value_part, query_doc_part, key_doc_part = members
        grouped = query_part.reshape(group_size, half_len, KV_HEADS, head_ratio, HEAD_DIM)
        scores = jnp.einsum(
            "gpkrd,glkd->gkrpl", grouped, key_part, preferred_element_type=jnp.float32
        )
        masked = jnp.where(visible(query_doc_part, key_doc_part), scores, masked_value)
        row_top = jnp.max(masked, axis=-1, keepdims=True)
        exponent = jnp.exp(masked - row_top)
        totals = jnp.sum(exponent, axis=-1, keepdims=True)
        weights = (exponent / totals).astype(jnp.bfloat16)
        mixed_part = jnp.einsum(
            "gkrpl,glkd->gpkrd", weights, value_part, preferred_element_type=jnp.float32
        )
        return (
            mixed_part.reshape(group_size, half_len, D).astype(jnp.bfloat16),
            row_top + jnp.log(totals),
        )

    mixed_blocks, log_totals = lax.map(
        attend,
        (
            blocks(queries),
            blocks(key_all),
            blocks(value_all),
            blocks(query_docs),
            blocks(documents),
        ),
    )
    mixed_heads = unblock(mixed_blocks)
    branch = jnp.einsum("spj,jd->spd", mixed_heads, out_rows, preferred_element_type=jnp.float32)
    residual_second = residual_first + branch
    inv_second = lax.rsqrt(
        jnp.mean(residual_second * residual_second, axis=-1, keepdims=True) + norm_epsilon
    )
    normal_second = residual_second * inv_second
    normed_second = (normal_second * gain_master[1]).astype(jnp.bfloat16)
    feed_inputs = lax.all_gather(normed_second, "narrow", axis=1, tiled=True)
    gate_values = jnp.einsum(
        "spd,ud->spu", feed_inputs, feedforward_half[0], preferred_element_type=jnp.float32
    )
    upward = jnp.einsum(
        "spd,ud->spu", feed_inputs, feedforward_half[1], preferred_element_type=jnp.float32
    )
    sigmoid_gate = jax.nn.sigmoid(gate_values)
    swish_gate = gate_values * sigmoid_gate
    hidden = (swish_gate * upward).astype(jnp.bfloat16)
    partial_out = jnp.einsum(
        "spu,ud->spd", hidden, feedforward_half[2], preferred_element_type=jnp.float32
    )
    feed_out = lax.psum_scatter(
        partial_out.astype(jnp.bfloat16), "narrow", scatter_dimension=1, tiled=True
    ).astype(jnp.float32)
    outputs = (residual_second + feed_out).astype(jnp.bfloat16)
    grad_rows = lax.all_gather(cotangent, "narrow", axis=1, tiled=True)
    grad_down = jnp.einsum("spu,spd->ud", hidden, grad_rows, preferred_element_type=jnp.float32)
    grad_hidden = jnp.einsum(
        "spd,ud->spu", grad_rows, feedforward_half[2], preferred_element_type=jnp.float32
    )
    grad_gate = (
        grad_hidden * upward * sigmoid_gate * (1.0 + gate_values * (1.0 - sigmoid_gate))
    ).astype(jnp.bfloat16)
    grad_upward = (grad_hidden * swish_gate).astype(jnp.bfloat16)
    grad_gate_rows = jnp.einsum(
        "spu,spd->ud", grad_gate, feed_inputs, preferred_element_type=jnp.float32
    )
    grad_up_rows = jnp.einsum(
        "spu,spd->ud", grad_upward, feed_inputs, preferred_element_type=jnp.float32
    )
    grad_feed_part = jnp.einsum(
        "spu,ud->spd", grad_gate, feedforward_half[0], preferred_element_type=jnp.float32
    )
    grad_feed_part = grad_feed_part + jnp.einsum(
        "spu,ud->spd", grad_upward, feedforward_half[1], preferred_element_type=jnp.float32
    )
    grad_normed_second = lax.psum_scatter(grad_feed_part, "narrow", scatter_dimension=1, tiled=True)
    feed_grad = jnp.stack([grad_gate_rows, grad_up_rows, grad_down])
    feedforward_grad = lax.psum_scatter(feed_grad, "wide", scatter_dimension=1, tiled=True)
    scaled_second = grad_normed_second * gain_master[1]
    gain_second_part = jnp.sum(grad_normed_second * normal_second, axis=(0, 1))
    grad_residual = cotangent.astype(jnp.float32) + inv_second * (
        scaled_second
        - normal_second * jnp.mean(scaled_second * normal_second, axis=-1, keepdims=True)
    )
    grad_branch = grad_residual.astype(jnp.bfloat16)
    grad_out_rows = jnp.einsum(
        "spj,spd->jd", mixed_heads, grad_branch, preferred_element_type=jnp.float32
    )
    grad_mixed = jnp.einsum(
        "spd,jd->spj", grad_branch, out_rows, preferred_element_type=jnp.float32
    ).astype(jnp.bfloat16)

    def attend_back(members):
        query_part, key_part, value_part, query_doc_part, key_doc_part, log_part, grad_part = (
            members
        )
        grouped = query_part.reshape(group_size, half_len, KV_HEADS, head_ratio, HEAD_DIM)
        scores = jnp.einsum(
            "gpkrd,glkd->gkrpl", grouped, key_part, preferred_element_type=jnp.float32
        )
        weights = jnp.exp(
            jnp.where(visible(query_doc_part, key_doc_part), scores, masked_value) - log_part
        )
        grad_grouped = grad_part.reshape(group_size, half_len, KV_HEADS, head_ratio, HEAD_DIM)
        grad_weights = jnp.einsum(
            "gpkrd,glkd->gkrpl", grad_grouped, value_part, preferred_element_type=jnp.float32
        )
        grad_value = jnp.einsum(
            "gkrpl,gpkrd->glkd",
            weights.astype(jnp.bfloat16),
            grad_grouped,
            preferred_element_type=jnp.float32,
        )
        inner_sum = jnp.sum(weights * grad_weights, axis=-1, keepdims=True)
        grad_scores = (weights * (grad_weights - inner_sum)).astype(jnp.bfloat16)
        grad_query = jnp.einsum(
            "gkrpl,glkd->gpkrd", grad_scores, key_part, preferred_element_type=jnp.float32
        )
        grad_key = jnp.einsum(
            "gkrpl,gpkrd->glkd", grad_scores, grouped, preferred_element_type=jnp.float32
        )
        return (grad_query.reshape(group_size, half_len, HEADS, HEAD_DIM), grad_key, grad_value)

    grad_query_blocks, grad_key_blocks, grad_value_blocks = lax.map(
        attend_back,
        (
            blocks(queries),
            blocks(key_all),
            blocks(value_all),
            blocks(query_docs),
            blocks(documents),
            log_totals,
            blocks(grad_mixed),
        ),
    )
    grad_key_own, grad_value_own = (
        lax.psum_scatter(
            unblock(grad_key_blocks).astype(jnp.bfloat16), "narrow", scatter_dimension=1, tiled=True
        ).astype(jnp.float32),
        lax.psum_scatter(
            unblock(grad_value_blocks).astype(jnp.bfloat16),
            "narrow",
            scatter_dimension=1,
            tiled=True,
        ).astype(jnp.float32),
    )
    grad_queries = rotate_back(
        unblock(grad_query_blocks) * HEAD_DIM ** (-0.5), cosine_table, sine_table
    ).astype(jnp.bfloat16)
    grad_keys = rotate_back(grad_key_own, cosine_table, sine_table).astype(jnp.bfloat16)
    grad_values = grad_value_own.astype(jnp.bfloat16)
    grad_projected = jnp.concatenate(
        [
            grad_queries.reshape(seq_count, half_len, D),
            grad_keys.reshape(seq_count, half_len, KV_WIDTH),
            grad_values.reshape(seq_count, half_len, KV_WIDTH),
        ],
        axis=-1,
    )
    grad_qkv_rows = jnp.einsum(
        "spj,spd->jd", grad_projected, normed_first, preferred_element_type=jnp.float32
    )
    grad_normed_first = jnp.einsum(
        "spj,jd->spd", grad_projected, qkv_rows, preferred_element_type=jnp.float32
    )
    attention_grad = lax.psum_scatter(
        jnp.concatenate([grad_qkv_rows, grad_out_rows], axis=0),
        ("wide", "narrow"),
        scatter_dimension=0,
        tiled=True,
    )
    scaled_first = grad_normed_first * gain_master[0]
    gain_first_part = jnp.sum(grad_normed_first * normal_first, axis=(0, 1))
    grad_tokens = grad_residual + inv_first * (
        scaled_first - normal_first * jnp.mean(scaled_first * normal_first, axis=-1, keepdims=True)
    )
    gain_grad = lax.psum(jnp.stack([gain_first_part, gain_second_part]), ("wide", "narrow"))
    local_squares = jnp.sum(attention_grad * attention_grad) + jnp.sum(
        feedforward_grad * feedforward_grad
    )
    grad_norm = jnp.sqrt(
        lax.psum(local_squares, ("wide", "narrow")) + jnp.sum(gain_grad * gain_grad)
    )
    factor = jnp.minimum(1.0, clip_limit / (grad_norm + 1e-06))
    attention_new, attention_first_new, attention_second_new = adamw_update(
        attention_master,
        attention_first,
        attention_second,
        attention_grad,
        factor,
        rate_matrix,
        weight_decay,
    )
    feedforward_new, feedforward_first_new, feedforward_second_new = adamw_update(
        feedforward_master,
        feedforward_first,
        feedforward_second,
        feedforward_grad,
        factor,
        rate_matrix,
        weight_decay,
    )
    gain_new, gain_first_new, gain_second_new = adamw_update(
        gain_master, gain_first, gain_second, gain_grad, factor, rate_gain, 0.0
    )
    return (
        outputs,
        grad_tokens,
        grad_norm,
        attention_new,
        attention_first_new,
        attention_second_new,
        feedforward_new,
        feedforward_first_new,
        feedforward_second_new,
        gain_new,
        gain_first_new,
        gain_second_new,
    )


def solution(mesh):
    in_specs = (
        P("wide", "narrow", None),
        P("wide", "narrow", None),
        P("wide", None),
        P(("wide", "narrow"), None),
        P(("wide", "narrow"), None),
        P(("wide", "narrow"), None),
        P(None, ("narrow", "wide"), None),
        P(None, ("narrow", "wide"), None),
        P(None, ("narrow", "wide"), None),
        P(),
        P(),
        P(),
    )
    out_specs = (
        P("wide", "narrow", None),
        P("wide", "narrow", None),
        P(),
        P(("wide", "narrow"), None),
        P(("wide", "narrow"), None),
        P(("wide", "narrow"), None),
        P(None, ("narrow", "wide"), None),
        P(None, ("narrow", "wide"), None),
        P(None, ("narrow", "wide"), None),
        P(),
        P(),
        P(),
    )
    return jax.shard_map(
        per_device, mesh=mesh, in_specs=in_specs, out_specs=out_specs, check_vma=False
    )
```

profile of v0, /device:TPU:0, one launch (start us, length us, event | category | flops | bytes accessed | tf_op | source)
XLA Modules:
  0.0 1017.7 jit_solution(16834755785406365379)
XLA Ops:
  12.4 57.9 %all-gather.7.cloned.1.call-done = bf16[1536,576]{1,0:T(8,128)(2,1)} async-done(((bf16[48,576]{1,0:T(8,128)(2,1)}), bf16[1536,576]{1,0:T(8,128)(2,1)}) %all-gather.7.cloned.1.call-update) | async-done | bytes 1769488 | tf_op jit(solution)/shard_map/all_gather | solution.py:93
  70.3 5.3 fusion.79
  75.7 3.1 copy-done.2
  88.6 13.1 %all-gather.11.cloned.1.call-done = bf16[4,1024,3,64]{1,3,2,0:T(8,128)(2,1)} async-done(((bf16[4,512,3,64]{1,3,2,0:T(8,128)(2,1)}), bf16[4,1024,3,64]{1,3,2,0:T(8,128)(2,1)}) %all-gather.11.cloned.1.call-update) | async-done | bytes 1572880 | tf_op jit(solution)/shard_map/all_gather | solution.py:126
  101.7 116.4 %while.28 = (s32[]{:T(128)}, bf16[4,1,512,576]{2,3,1,0:T(8,128)(2,1)}, f32[4,1,3,3,512,1]{4,3,2,5,1,0:T(4,128)S(1)}, bf16[4,1,1024,3,64]{2,4,3,1,0:T(8,128)(2,1)...) while((s32[]{:T(128)}, ...), condition=%wide.region_4.5_spmd.clone, body=%wide.region_1.4_spmd.clone.sunk | while | flops 1252290048 | bytes 63232136 | solution.py:162
  102.3 9.1 fusion.141
  111.4 9.8 fusion.142
  121.1 8.8 fusion.143
  131.4 9.1 fusion.141
  140.5 9.6 fusion.142
  150.1 9.2 fusion.143
  160.8 9.1 fusion.141
  169.9 9.6 fusion.142
  179.5 8.8 fusion.143
  189.8 9.1 fusion.141
  198.9 9.6 fusion.142
  208.4 8.8 fusion.143
  218.2 4.9 multiply_reduce_fusion.2
  228.0 14.9 %all-gather.13.cloned.1.call-done = bf16[4,1024,576]{1,2,0:T(8,128)(2,1)} async-done(((bf16[4,512,576]{1,2,0:T(8,128)(2,1)}), bf16[4,1024,576]{1,2,0:T(8,128)(2,1)}) %all-gather.13.cloned.1.call-update) | async-done | bytes 4718608 | tf_op jit(solution)/shard_map/all_gather | solution.py:180
  243.0 10.5 %fusion.82 = f32[4,1024,768]{2,1,0:T(8,128)} fusion(bf16[4,1024,576]{1,2,0:T(8,128)(2,1)} %all-gather.13.cloned.1.call-done, bf16[3,768,576]{2,1,0:T(8,128)(2,1)} %all-gather.15.cloned.1.call-done), kind=kOutput, calls=%fused_computation.126 | convolution fusion | flops 3623878656 | bytes 18284544 | tf_op jit(solution)/shard_map/spd,ud->spu/dot_general | solution.py:184
  253.5 9.5 fusion.81
  263.0 19.3 %multiply_convert_fusion = (bf16[4,1024,768]{2,1,0:T(8,128)(2,1)}, bf16[4,1024,768]{2,1,0:T(8,128)(2,1)}, bf16[4,1024,768]{2,1,0:T(8,128)(2,1)}) fusion(f32[4,1024,768]{2,1,0:T(8,128)} %fusion.81, f32[4,1024,768]{2,1,0:T(8,128)} %fusion.82, bf16[4,1024,576]{1,2,0:T(8,128)(2,1)} %all-gather.17.cloned.1.call-done, ...), kind=kOutput, calls=%fused_computation.63 | convolution fusion | flops 3671064576 | bytes 49741824 | tf_op jit(solution)/shard_map/spd,ud->spu/dot_general | solution.py:199
  282.3 7.5 fusion.80
  289.8 11.0 %convolution_add_fusion = f32[4,1024,576]{1,2,0:T(8,128)} fusion(f32[4,1024,576]{1,2,0:T(8,128)S(1)} %fusion.80, bf16[4,1024,768]{2,1,0:T(8,128)(2,1)} %get-tuple-element.329, bf16[3,768,576]{2,1,0:T(8,128)(2,1)} %all-gather.15.cloned.1.call-done), kind=kOutput, calls=%fused_computation.95 | convolution fusion | flops 3626237952 | bytes 26148864 | tf_op jit(solution)/shard_map/spu,ud->spd/dot_general | solution.py:215
  300.9 9.0 convolution_convert_fusion
  310.0 10.0 reduce-scatter.10.cloned.1.call-done
  320.0 5.6 multiply_reduce_fusion
  325.6 10.5 %reduce-scatter.8.cloned.1.call-done = bf16[4,512,576]{1,2,0:T(8,128)(2,1)} async-done(((bf16[4,1024,576]{1,2,0:T(8,128)(2,1)}), bf16[4,512,576]{1,2,0:T(8,128)(2,1)}) %reduce-scatter.8.cloned.1.call-update) | async-done | bytes 2359312 | tf_op jit(solution)/shard_map/reduce_scatter | solution.py:193
  336.2 7.7 multiply_add_fusion
  346.1 4.6 convert_bitcast_fusion
  350.6 214.0 %while.29 = (s32[]{:T(128)}, f32[4,1,512,9,64]{2,4,3,1,0:T(8,128)}, bf16[4,1,1024,3,64]{2,4,3,1,0:T(8,128)(2,1)}, bf16[4,1,1024,3,64]{2,4,3,1,0:T(8,128)(2,1)}, ...) while((s32[]{:T(128)}, f32[4,1,512,9,64]{2,4,3,1,0:T(8,128)}, ...), condition=%wide.region_11.12_spmd.clone, body=%wide.region_9.11_spmd.clone.sunk | while | flops 3078090240 | bytes 179986704 | solution.py:266
  352.3 9.1 fusion.153
  361.4 8.6 fusion.159
  370.1 13.4 %fusion.155 = (f32[3,3,512]{2,1,0:T(4,128)S(1)}, f32[3,1024,512,3]{2,1,3,0:T(8,128)}) fusion(f32[3,1024,512,3]{2,1,3,0:T(8,128)} %fusion.153, f32[3,3,512]{2,1,0:T(4,128)S(1)} %dynamic-slice_bitcast_fusion.2, pred[512,1024]{0,1:T(8,128)(4,1)S(1)} %fusion.154, bf16[512,3,3,64]{0,3,2,1:T(8,128)(2,1)S(1)} %bitcast.338, ...), kind=kOutput, calls=%fused_computation.30.clone.1 | convolution fusion | flops 622849536 | bytes 39292932 | tf_op jit(solution)/shard_map/while/body/eval_jaxpr/gpkrd,glkd->gkrpl/dot_general | solution.py:247
  383.5 13.6 %fusion.156 = bf16[3,3,512,1024]{2,3,1,0:T(8,128)(2,1)S(1)} fusion(f32[3,1024,512,3]{2,1,3,0:T(8,128)} %get-tuple-element.481, f32[3,1024,512,3]{2,1,3,0:T(8,128)} %fusion.153, f32[3,3,512]{2,1,0:T(4,128)S(1)} %get-tuple-element.482, f32[3,3,512]{2,1,0:T(4,128)S(1)} %dynamic-slice_bitcast_fusion.2, pred[512,1024]{0,1:T(8,128)(4,1)S(1)} %fusion.154), kind=kLoop, calls=%fused_computation.35.clone.1 | loop fusion | flops 23592960 | bytes 47747072 | tf_op jit(solution)/shard_map/reshape.54
  400.0 3.0 fusion.157
  405.8 9.1 fusion.153
  414.9 8.6 fusion.159
  423.5 13.4 %fusion.155 = (f32[3,3,512]{2,1,0:T(4,128)S(1)}, f32[3,1024,512,3]{2,1,3,0:T(8,128)}) fusion(f32[3,1024,512,3]{2,1,3,0:T(8,128)} %fusion.153, f32[3,3,512]{2,1,0:T(4,128)S(1)} %dynamic-slice_bitcast_fusion.2, pred[512,1024]{0,1:T(8,128)(4,1)S(1)} %fusion.154, bf16[512,3,3,64]{0,3,2,1:T(8,128)(2,1)S(1)} %bitcast.338, ...), kind=kOutput, calls=%fused_computation.30.clone.1 | convolution fusion | flops 622849536 | bytes 39292932 | tf_op jit(solution)/shard_map/while/body/eval_jaxpr/gpkrd,glkd->gkrpl/dot_general | solution.py:247
  436.9 13.6 %fusion.156 = bf16[3,3,512,1024]{2,3,1,0:T(8,128)(2,1)S(1)} fusion(f32[3,1024,512,3]{2,1,3,0:T(8,128)} %get-tuple-element.481, f32[3,1024,512,3]{2,1,3,0:T(8,128)} %fusion.153, f32[3,3,512]{2,1,0:T(4,128)S(1)} %get-tuple-element.482, f32[3,3,512]{2,1,0:T(4,128)S(1)} %dynamic-slice_bitcast_fusion.2, pred[512,1024]{0,1:T(8,128)(4,1)S(1)} %fusion.154), kind=kLoop, calls=%fused_computation.35.clone.1 | loop fusion | flops 23592960 | bytes 47747072 | tf_op jit(solution)/shard_map/reshape.54
  453.5 3.0 fusion.157
  459.3 9.1 fusion.153
  468.4 8.6 fusion.159
  477.1 13.4 %fusion.155 = (f32[3,3,512]{2,1,0:T(4,128)S(1)}, f32[3,1024,512,3]{2,1,3,0:T(8,128)}) fusion(f32[3,1024,512,3]{2,1,3,0:T(8,128)} %fusion.153, f32[3,3,512]{2,1,0:T(4,128)S(1)} %dynamic-slice_bitcast_fusion.2, pred[512,1024]{0,1:T(8,128)(4,1)S(1)} %fusion.154, bf16[512,3,3,64]{0,3,2,1:T(8,128)(2,1)S(1)} %bitcast.338, ...), kind=kOutput, calls=%fused_computation.30.clone.1 | convolution fusion | flops 622849536 | bytes 39292932 | tf_op jit(solution)/shard_map/while/body/eval_jaxpr/gpkrd,glkd->gkrpl/dot_general | solution.py:247
  490.4 13.6 %fusion.156 = bf16[3,3,512,1024]{2,3,1,0:T(8,128)(2,1)S(1)} fusion(f32[3,1024,512,3]{2,1,3,0:T(8,128)} %get-tuple-element.481, f32[3,1024,512,3]{2,1,3,0:T(8,128)} %fusion.153, f32[3,3,512]{2,1,0:T(4,128)S(1)} %get-tuple-element.482, f32[3,3,512]{2,1,0:T(4,128)S(1)} %dynamic-slice_bitcast_fusion.2, pred[512,1024]{0,1:T(8,128)(4,1)S(1)} %fusion.154), kind=kLoop, calls=%fused_computation.35.clone.1 | loop fusion | flops 23592960 | bytes 47747072 | tf_op jit(solution)/shard_map/reshape.54
  507.0 3.0 fusion.157
  512.8 9.1 fusion.153
  521.9 8.6 fusion.159
  530.6 13.4 %fusion.155 = (f32[3,3,512]{2,1,0:T(4,128)S(1)}, f32[3,1024,512,3]{2,1,3,0:T(8,128)}) fusion(f32[3,1024,512,3]{2,1,3,0:T(8,128)} %fusion.153, f32[3,3,512]{2,1,0:T(4,128)S(1)} %dynamic-slice_bitcast_fusion.2, pred[512,1024]{0,1:T(8,128)(4,1)S(1)} %fusion.154, bf16[512,3,3,64]{0,3,2,1:T(8,128)(2,1)S(1)} %bitcast.338, ...), kind=kOutput, calls=%fused_computation.30.clone.1 | convolution fusion | flops 622849536 | bytes 39292932 | tf_op jit(solution)/shard_map/while/body/eval_jaxpr/gpkrd,glkd->gkrpl/dot_general | solution.py:247
  543.9 13.6 %fusion.156 = bf16[3,3,512,1024]{2,3,1,0:T(8,128)(2,1)S(1)} fusion(f32[3,1024,512,3]{2,1,3,0:T(8,128)} %get-tuple-element.481, f32[3,1024,512,3]{2,1,3,0:T(8,128)} %fusion.153, f32[3,3,512]{2,1,0:T(4,128)S(1)} %get-tuple-element.482, f32[3,3,512]{2,1,0:T(4,128)S(1)} %dynamic-slice_bitcast_fusion.2, pred[512,1024]{0,1:T(8,128)(4,1)S(1)} %fusion.154), kind=kLoop, calls=%fused_computation.35.clone.1 | loop fusion | flops 23592960 | bytes 47747072 | tf_op jit(solution)/shard_map/reshape.54
  560.5 3.0 fusion.157
  565.3 8.8 convolution_bitcast_fusion.2
  574.2 8.7 convolution_bitcast_fusion.3
  583.0 3.9 convolution_bitcast_fusion.4
  589.6 8.9 copy.94
  598.6 3.1 fusion.65
  605.8 3.2 fusion.74
  611.8 4.7 convolution_bitcast_fusion.1
  617.1 3.1 copy.109
  622.3 221.7 %all-reduce.4.cloned.1.call-done = f32[3,768,576]{2,0,1:T(4,128)} async-done(((f32[3,768,576]{2,0,1:T(4,128)}), f32[3,768,576]{2,0,1:T(4,128)}) %all-reduce.4.cloned.1.call-update) | async-done | bytes 5308432
  845.9 8.0 fusion.62
  853.9 98.4 %reduce-scatter.16.cloned.1.call-done = f32[48,576]{1,0:T(8,128)} async-done(((f32[1536,576]{1,0:T(8,128)}), f32[48,576]{1,0:T(8,128)}) %reduce-scatter.16.cloned.1.call-update) | async-done | bytes 110608 | tf_op jit(solution)/shard_map/reduce_scatter | solution.py:308
  955.4 7.5 fusion.61
  962.8 40.1 %all-reduce.1 = (f32[]{:T(128)}, f32[2,576]{1,0:T(2,128)S(1)}) all-reduce(f32[]{:T(128)S(6)} %add.163, f32[2,576]{1,0:T(2,128)S(1)} %pad_maximum_fusion.8), channel_id=1, replica_groups=mesh['wide'=16,'narrow'=2] {'wide','narrow'}, use_global_device_ids=true, to_apply=%region_19.20 | all-reduce | flops 1153 | bytes 9224 | tf_op jit(solution)/shard_map/psum | solution.py:324
  (233 shorter events, 71.9 us)
Async XLA Ops:
  7.2 63.2 %all-gather.7.cloned.1.call-start = ((), (), s32[]{:S(2)}) async-start(), calls=%async_computation.5 | async-start | bytes 2027520 | tf_op jit(solution)/shard_map/all_gather | solution.py:93
  8.8 79.8 %all-gather.9.cloned.1.call-start = ((), (), s32[]{:S(2)}) async-start(), calls=%async_computation.6 | async-start | bytes 2359296 | tf_op jit(solution)/shard_map/all_gather | solution.py:127
  10.2 65.5 %copy-start.25 = (f32[576]{0:T(1024)}, f32[576]{0:T(1024)S(1)}, u32[]{:S(2)}) copy-start(f32[576]{0:T(1024)S(1)} %get-tuple-element.269) | copy-start | bytes 6916
  12.4 63.3 %copy-start.21 = (f32[4,512]{1,0:T(4,128)}, f32[4,512]{1,0:T(4,128)S(1)}, u32[]{:S(2)}) copy-start(f32[4,512]{1,0:T(4,128)S(1)} %add_rsqrt_fusion.1) | copy-start | bytes 24580
  75.7 3.1 copy-start.2
  79.8 1.5 slice-start.2
  79.8 2.7 copy-start.14
  79.8 4.0 copy-start.20
  79.8 21.9 %all-gather.11.cloned.1.call-start = ((), (), s32[]{:S(2)}) async-start(), calls=%async_computation.7 | async-start | bytes 2359296 | tf_op jit(solution)/shard_map/all_gather | solution.py:126
  80.2 3.7 copy-start.5
  80.2 3.7 copy-start.7
  82.5 145.6 %all-gather.15.cloned.1.call-start = ((), (), s32[]{:S(2)}) async-start(), calls=%async_computation.9 | async-start | bytes 3133440 | tf_op jit(solution)/shard_map/all_gather | solution.py:96
  83.2 159.7 %all-gather.13.cloned.1.call-start = ((), (), s32[]{:S(2)}) async-start(), calls=%async_computation.8 | async-start | bytes 7077888 | tf_op jit(solution)/shard_map/all_gather | solution.py:180
  83.8 2.7 slice-start.3
  218.2 7.1 copy-start.19
  223.1 2.2 copy-start
  227.2 35.8 %all-gather.17.cloned.1.call-start = ((), (), s32[]{:S(2)}) async-start(), calls=%async_computation.11 | async-start | bytes 7077888 | tf_op jit(solution)/shard_map/all_gather | solution.py:197
  227.8 92.2 %reduce-scatter.10.cloned.1.call-start = ((), (), s32[]{:S(2)}) async-start(), calls=%async_computation.12 | async-start | bytes 14155776 | tf_op jit(solution)/shard_map/reduce_scatter | solution.py:218
  243.0 10.5 %copy-start.29 = (bf16[4,1024,576]{1,2,0:T(8,128)(2,1)S(1)}, bf16[4,1024,576]{1,2,0:T(8,128)(2,1)}, u32[]{:S(2)}) copy-start(bf16[4,1024,576]{1,2,0:T(8,128)(2,1)} %all-gather.13.cloned.1.call-done) | copy-start | bytes 14155780
  300.8 35.4 %reduce-scatter.8.cloned.1.call-start = ((), (), s32[]{:S(2)}) async-start(), calls=%async_computation.10 | async-start | bytes 7077888 | tf_op jit(solution)/shard_map/reduce_scatter | solution.py:193
  309.9 299.1 %reduce-scatter.12.cloned.1.call-start = ((), (), s32[]{:S(2)}) async-start(), calls=%async_computation.13 | async-start | bytes 2359296 | tf_op jit(solution)/shard_map/reduce_scatter | solution.py:279
  343.9 2.2 copy-start.1
  352.3 9.1 copy-start.9
  370.1 13.4 %copy-start.10 = (bf16[4,1,1024,3,64]{2,4,3,1,0:T(8,128)(2,1)}, bf16[4,1,1024,3,64]{2,4,3,1,0:T(8,128)(2,1)S(1)}, u32[]{:S(2)}) copy-start(bf16[4,1,1024,3,64]{2,4,3,1,0:T(8,128)(2,1)S(1)} %fusion.159) | copy-start | bytes 4718596 | tf_op jit(solution)/shard_map/while
  383.4 13.6 %copy-start.11 = (bf16[4,1,1024,3,64]{2,4,3,1,0:T(8,128)(2,1)S(1)}, bf16[4,1,1024,3,64]{2,4,3,1,0:T(8,128)(2,1)}, u32[]{:S(2)}) copy-start(bf16[4,1,1024,3,64]{2,4,3,1,0:T(8,128)(2,1)} %get-tuple-element.528) | copy-start | bytes 4718596 | tf_op jit(solution)/shard_map/while
  400.0 3.0 copy-start.12
  405.8 9.1 copy-start.9
  423.5 13.4 %copy-start.10 = (bf16[4,1,1024,3,64]{2,4,3,1,0:T(8,128)(2,1)}, bf16[4,1,1024,3,64]{2,4,3,1,0:T(8,128)(2,1)S(1)}, u32[]{:S(2)}) copy-start(bf16[4,1,1024,3,64]{2,4,3,1,0:T(8,128)(2,1)S(1)} %fusion.159) | copy-start | bytes 4718596 | tf_op jit(solution)/shard_map/while
  436.9 13.6 %copy-start.11 = (bf16[4,1,1024,3,64]{2,4,3,1,0:T(8,128)(2,1)S(1)}, bf16[4,1,1024,3,64]{2,4,3,1,0:T(8,128)(2,1)}, u32[]{:S(2)}) copy-start(bf16[4,1,1024,3,64]{2,4,3,1,0:T(8,128)(2,1)} %get-tuple-element.528) | copy-start | bytes 4718596 | tf_op jit(solution)/shard_map/while
  453.5 3.0 copy-start.12
  459.3 9.1 copy-start.9
  477.0 13.4 %copy-start.10 = (bf16[4,1,1024,3,64]{2,4,3,1,0:T(8,128)(2,1)}, bf16[4,1,1024,3,64]{2,4,3,1,0:T(8,128)(2,1)S(1)}, u32[]{:S(2)}) copy-start(bf16[4,1,1024,3,64]{2,4,3,1,0:T(8,128)(2,1)S(1)} %fusion.159) | copy-start | bytes 4718596 | tf_op jit(solution)/shard_map/while
  490.4 13.6 %copy-start.11 = (bf16[4,1,1024,3,64]{2,4,3,1,0:T(8,128)(2,1)S(1)}, bf16[4,1,1024,3,64]{2,4,3,1,0:T(8,128)(2,1)}, u32[]{:S(2)}) copy-start(bf16[4,1,1024,3,64]{2,4,3,1,0:T(8,128)(2,1)} %get-tuple-element.528) | copy-start | bytes 4718596 | tf_op jit(solution)/shard_map/while
  507.0 3.0 copy-start.12
  512.8 9.1 copy-start.9
  530.6 13.4 %copy-start.10 = (bf16[4,1,1024,3,64]{2,4,3,1,0:T(8,128)(2,1)}, bf16[4,1,1024,3,64]{2,4,3,1,0:T(8,128)(2,1)S(1)}, u32[]{:S(2)}) copy-start(bf16[4,1,1024,3,64]{2,4,3,1,0:T(8,128)(2,1)S(1)} %fusion.159) | copy-start | bytes 4718596 | tf_op jit(solution)/shard_map/while
  543.9 13.6 %copy-start.11 = (bf16[4,1,1024,3,64]{2,4,3,1,0:T(8,128)(2,1)S(1)}, bf16[4,1,1024,3,64]{2,4,3,1,0:T(8,128)(2,1)}, u32[]{:S(2)}) copy-start(bf16[4,1,1024,3,64]{2,4,3,1,0:T(8,128)(2,1)} %get-tuple-element.528) | copy-start | bytes 4718596 | tf_op jit(solution)/shard_map/while
  560.5 3.0 copy-start.12
  564.6 46.2 %reduce-scatter.14.cloned.1.call-start = ((), (), s32[]{:S(2)}) async-start(), calls=%async_computation.14 | async-start | bytes 2359296 | tf_op jit(solution)/shard_map/reduce_scatter | solution.py:282
  565.2 278.8 %all-reduce.4.cloned.1.call-start = ((), (), s32[]{:S(2)}) async-start(), calls=%async_computation.16 | async-start | bytes 15728640
  565.3 17.6 %slice-start.4 = ((s8[4718592]{0:T(1024)(128)(4,1)}), s8[4194304]{0:T(1024)(128)(4,1)S(1)}, s32[]{:S(2)}) async-start(s8[4718592]{0:T(1024)(128)(4,1)} %bitcast.357), calls=%async_computation.21 | async-start | bytes 8388608
  565.3 17.6 %slice-start.6 = ((s8[6291456]{0:T(1024)(128)(4,1)}), s8[4194304]{0:T(1024)(128)(4,1)S(1)}, s32[]{:S(2)}) async-start(s8[6291456]{0:T(1024)(128)(4,1)} %bitcast.361), calls=%async_computation.23 | async-start | bytes 8388608
  574.1 8.8 slice-start.5
  574.2 8.8 slice-start.7
  598.5 353.7 %reduce-scatter.16.cloned.1.call-start = ((), (), s32[]{:S(2)}) async-start(), calls=%async_computation.15 | async-start | bytes 4055040 | tf_op jit(solution)/shard_map/reduce_scatter | solution.py:308
  598.6 3.2 copy-start.6
  598.6 3.2 copy-start.8
  598.6 5.6 slice-start
  601.8 2.8 slice-start.1
  601.8 4.0 copy-start.30
  609.0 2.8 copy-start.3
  609.0 2.8 copy-start.22
  609.0 2.8 copy-start.26
  610.8 0.9 copy-start.16
  611.8 4.7 copy-start.13
  617.1 228.8 %copy-start.24 = (f32[576]{0:T(1024)S(1)}, f32[576]{0:T(1024)}, u32[]{:S(2)}) copy-start(f32[576]{0:T(1024)} %get-tuple-element.264) | copy-start | bytes 6916
  620.2 225.7 %copy-start.4 = (bf16[4,512,576]{1,2,0:T(8,128)(2,1)S(1)}, bf16[4,512,576]{1,2,0:T(8,128)(2,1)}, u32[]{:S(2)}) copy-start(bf16[4,512,576]{1,2,0:T(8,128)(2,1)} %param.16) | copy-start | bytes 7077892
  955.3 49.6 %copy-start.23 = (f32[2,576]{1,0:T(2,128)S(1)}, f32[2,576]{1,0:T(2,128)}, u32[]{:S(2)}) copy-start(f32[2,576]{1,0:T(2,128)} %param.25) | copy-start | bytes 13828
  955.3 49.6 %copy-start.27 = (f32[2,576]{1,0:T(2,128)S(1)}, f32[2,576]{1,0:T(2,128)}, u32[]{:S(2)}) copy-start(f32[2,576]{1,0:T(2,128)} %param.26) | copy-start | bytes 13828
  955.3 49.6 %copy-start.28 = (f32[2,576]{1,0:T(2,128)S(1)}, f32[2,576]{1,0:T(2,128)}, u32[]{:S(2)}) copy-start(f32[2,576]{1,0:T(2,128)} %param.27) | copy-start | bytes 13828
  955.3 50.2 %copy-start.15 = (f32[3,48,576]{2,1,0:T(8,128)S(1)}, f32[3,48,576]{2,1,0:T(8,128)}, u32[]{:S(2)}) copy-start(f32[3,48,576]{2,1,0:T(8,128)} %param.22) | copy-start | bytes 995332
  955.4 52.4 %copy-start.17 = (f32[48,576]{1,0:T(8,128)S(1)}, f32[48,576]{1,0:T(8,128)}, u32[]{:S(2)}) copy-start(f32[48,576]{1,0:T(8,128)} %param.19) | copy-start | bytes 331780
  955.4 52.4 %copy-start.18 = (f32[48,576]{1,0:T(8,128)S(1)}, f32[48,576]{1,0:T(8,128)}, u32[]{:S(2)}) copy-start(f32[48,576]{1,0:T(8,128)} %reduce-scatter.16.cloned.1.call-done) | copy-start | bytes 331780
Sparse Core Ops, SparseCore 0:
  11.5 58.7 all-gather.6
  79.9 8.6 all-gather.8
  90.7 10.9 all-gather.10
  104.8 67.4 all-gather.14
  227.3 15.5 all-gather.12
  244.4 15.6 all-gather.16
  300.9 19.0 reduce-scatter.9
  322.3 13.8 reduce-scatter.7
  564.8 10.1 reduce-scatter.11
  577.1 10.2 reduce-scatter.13
  598.6 245.3 all-reduce.3
  849.3 102.9 reduce-scatter.15
where the time goes:
time: 1020 us
  waiting for transfers between devices  428 us (42%)
  matrix products  339 us (33%)
  other arithmetic  146 us (14%)
  local copies, waits for them, and re-layouts  43.7 us (4%)
  blocking collectives  40.1 us (4%)
  between operations  19.5 us (2%)
    unnamed x13, waiting for transfers between devices  223 us
    reduce_scatter x1, waiting for transfers between devices, per_device(): lax.psum_scatter(jnp.concatenate([grad_qkv_rows, grad_out_rows], axis=0),...  98.4 us
    all_gather x1, waiting for transfers between devices, per_device(): lax.all_gather(attention_master.astype(jnp.bfloat16), ('wide', 'narrow'),...  57.9 us
    another operation x9, other arithmetic  55.6 us
    dot_general x4, matrix products, attend_back(): jnp.einsum('gpkrd,glkd->gkrpl', grad_grouped, value_part, preferred_eleme...  53.5 us
    psum x1, blocking collectives, per_device(): lax.psum(local_squares, ('wide', 'narrow')) + jnp.sum(gain_grad * gain_grad)  40.1 us
    reduce_sum x4, other arithmetic, attend(): totals = jnp.sum(exponent, axis=-1, keepdims=True)  38.5 us
    dot_general x4, matrix products, attend_back(): jnp.einsum('gpkrd,glkd->gkrpl', grouped, key_part, preferred_element_type...  36.4 us
  transfers between devices with their start and end apart: 12, of which 8 were waited for; matrix products, arithmetic and copies ran while one was open for 22% of the time, Pallas kernels for 0%

commit v1 on v0

v1 whole, which is shorter than its diff:
```python
import functools

import jax
import jax.numpy as jnp
import numpy as np
from jax import lax
from jax.experimental import pallas as pl
from jax.experimental.pallas import tpu as pltpu
from jax.sharding import PartitionSpec as P

D = 576
HEADS = 9
KV_HEADS = 3
RATIO = 3
HEAD_DIM = 64
HALF = 32
STEP = 10
KV_WIDTH = 192
QKV = 960
BLOCK = 256

norm_epsilon = 1e-05
adam_epsilon = 1e-08
beta_first = 0.9
beta_second = 0.999
weight_decay = 0.1
rate_matrix = 0.05
rate_gain = 0.5
clip_limit = 1.0
rotary_base = 10000.0
masked_value = -1e30

F32 = jnp.float32
BF16 = jnp.bfloat16
VMEM_LIMIT = 60 * 2**20


def rotary_tables(length):
    frequency = np.float32(rotary_base) ** (
        np.float32(-2.0) * np.arange(HALF, dtype=np.float32) / np.float32(HEAD_DIM)
    )
    angles = np.arange(length, dtype=np.float32)[None, :] * frequency.astype(np.float32)[:, None]
    return jnp.asarray(np.cos(angles), F32), jnp.asarray(np.sin(angles), F32)


def dot(left, right, left_dim=1, right_dim=0):
    return lax.dot_general(
        left, right, (((left_dim,), (right_dim,)), ((), ())), preferred_element_type=F32
    )


def inverse_root(values):
    return lax.rsqrt(jnp.mean(values * values, axis=-1, keepdims=True) + norm_epsilon)


def visible_scores(scores, start_row, place_row, query_block):
    parts = []
    for key_block in range(query_block + 1):
        part = scores[key_block * BLOCK : (key_block + 1) * BLOCK]
        place = lax.broadcasted_iota(jnp.int32, part.shape, 0) + key_block * BLOCK
        seen = place >= start_row
        if key_block == query_block:
            seen = seen & (place <= place_row)
        parts.append(jnp.where(seen, part, masked_value))
    return jnp.concatenate(parts, axis=0) if len(parts) > 1 else parts[0]


def triple(row):
    return jnp.concatenate([row] * RATIO, axis=1)


def attention_forward_body(
    x_ref,
    start_ref,
    weight_ref,
    gain_ref,
    cosine_ref,
    sine_ref,
    residual_ref,
    query_ref,
    key_ref,
    value_ref,
    mixed_ref,
    total_ref,
    key_rows,
):
    length = x_ref.shape[1]
    x = x_ref[0].astype(F32)
    normed = (x * inverse_root(x) * gain_ref[0:1]).astype(BF16)
    cosine = cosine_ref[...]
    sine = sine_ref[...]
    projected = dot(weight_ref[0:QKV], normed, 1, 1)
    for head in range(HEADS):
        front = projected[head * 64 : head * 64 + 32]
        behind = projected[head * 64 + 32 : head * 64 + 64]
        query_ref[0, head * 64 : head * 64 + 32] = (
            (front * cosine - behind * sine) * HEAD_DIM ** (-0.5)
        ).astype(BF16)
        query_ref[0, head * 64 + 32 : head * 64 + 64] = (
            (behind * cosine + front * sine) * HEAD_DIM ** (-0.5)
        ).astype(BF16)
    for head in range(KV_HEADS):
        base = D + head * 64
        front = projected[base : base + 32]
        behind = projected[base + 32 : base + 64]
        rotated = jnp.concatenate(
            [front * cosine - behind * sine, behind * cosine + front * sine], axis=0
        )
        key_ref[0, head * 64 : head * 64 + 64] = rotated.astype(BF16)
        key_rows[head] = rotated.T.astype(BF16)
    value_ref[0] = projected[D + KV_WIDTH :].astype(BF16)

    def group(member, carry):
        for block in range(length // BLOCK):
            low, high = block * BLOCK, (block + 1) * BLOCK
            queries = jnp.concatenate(
                [
                    query_ref[0, pl.ds(member * 192 + r * 64, 64), low:high]
                    for r in range(RATIO)
                ],
                axis=1,
            )
            scores = dot(key_rows[member, 0:high], queries)
            start_row = triple(start_ref[0, 0:1, low:high])
            place_row = triple(lax.broadcasted_iota(jnp.int32, (1, BLOCK), 1) + low)
            scores = visible_scores(scores, start_row, place_row, block)
            top = jnp.max(scores, axis=0, keepdims=True)
            exponent = jnp.exp(scores - top)
            total = jnp.sum(exponent, axis=0, keepdims=True)
            values = value_ref[0, pl.ds(member * 64, 64), 0:high]
            mixed = dot(values, exponent.astype(BF16)) * (1.0 / total)
            log_total = top + jnp.log(total)
            for r in range(RATIO):
                lanes = slice(r * BLOCK, (r + 1) * BLOCK)
                mixed_ref[0, pl.ds(member * 192 + r * 64, 64), low:high] = mixed[:, lanes].astype(
                    BF16
                )
                total_ref[0, member, r : r + 1, low:high] = log_total[:, lanes]
        return carry

    lax.fori_loop(0, KV_HEADS, group, 0)
    branch = dot(mixed_ref[0].T, weight_ref[QKV:])
    residual_ref[0] = x_ref[0].astype(F32) + branch


def whole(shape):
    return pl.BlockSpec(shape, lambda *_: (0,) * len(shape))


def row_block(shape):
    return pl.BlockSpec((1,) + shape, lambda s: (s,) + (0,) * len(shape))


def params():
    return pltpu.CompilerParams(
        dimension_semantics=("arbitrary",), vmem_limit_bytes=VMEM_LIMIT
    )


def attention_forward(x, start, weights, gain, tables):
    count, length, _ = x.shape
    outs = [
        ((length, D), F32),
        ((D, length), BF16),
        ((KV_WIDTH, length), BF16),
        ((KV_WIDTH, length), BF16),
        ((D, length), BF16),
        ((KV_HEADS, 8, length), F32),
    ]
    return pl.pallas_call(
        attention_forward_body,
        grid=(count,),
        in_specs=[
            row_block((length, D)),
            row_block((1, length)),
            whole(weights.shape),
            whole(gain.shape),
            whole((HALF, length)),
            whole((HALF, length)),
        ],
        out_specs=[row_block(shape) for shape, _ in outs],
        out_shape=[jax.ShapeDtypeStruct((count,) + shape, kind) for shape, kind in outs],
        scratch_shapes=[pltpu.VMEM((KV_HEADS, length, HEAD_DIM), BF16)],
        compiler_params=params(),
        cost_estimate=pl.CostEstimate(
            flops=8_000_000_000, transcendentals=12_000_000, bytes_accessed=20_000_000
        ),
        name="attention_forward",
    )(x, start, weights, gain, *tables)


def feed_body(
    residual_ref,
    cotangent_ref,
    own_ref,
    other_ref,
    gain_ref,
    out_ref,
    back_ref,
    own_grad_ref,
    other_grad_ref,
    gain_grad_ref,
    sums,
):
    step = pl.program_id(0)
    units = own_ref.shape[1]
    residual = residual_ref[...]
    cotangent = cotangent_ref[...]
    gain = gain_ref[1:2]
    inverse = inverse_root(residual)
    normal = residual * inverse
    normed = (normal * gain).astype(BF16)
    normed_across = normed.T
    cotangent_across = cotangent.T

    @pl.when(step == 0)
    def _():
        sums[...] = jnp.zeros_like(sums)
        gain_grad_ref[...] = jnp.zeros_like(gain_grad_ref)

    out = residual
    grad_normed = jnp.zeros_like(residual)
    for part, weight_ref in enumerate((own_ref, other_ref)):
        lanes = slice(part * units, (part + 1) * units)
        gate = dot(normed, weight_ref[0], 1, 1)
        upward = dot(normed, weight_ref[1], 1, 1)
        sigmoid_gate = jax.nn.sigmoid(gate)
        swish = gate * sigmoid_gate
        hidden = (swish * upward).astype(BF16)
        out = out + dot(hidden, weight_ref[2])
        grad_hidden = dot(cotangent, weight_ref[2], 1, 1)
        grad_gate = (
            grad_hidden * upward * sigmoid_gate * (1.0 + gate * (1.0 - sigmoid_gate))
        ).astype(BF16)
        grad_upward = (grad_hidden * swish).astype(BF16)
        grad_normed = (
            grad_normed + dot(grad_gate, weight_ref[0]) + dot(grad_upward, weight_ref[1])
        )
        sums[0, :, lanes] += dot(normed_across, grad_gate)
        sums[1, :, lanes] += dot(normed_across, grad_upward)
        sums[2, :, lanes] += dot(cotangent_across, hidden)
    out_ref[...] = out.astype(BF16)
    scaled = grad_normed * gain
    gain_grad_ref[...] += jnp.sum(grad_normed * normal, axis=0, keepdims=True)
    back_ref[...] = cotangent.astype(F32) + inverse * (
        scaled - normal * jnp.mean(scaled * normal, axis=-1, keepdims=True)
    )

    @pl.when(step == pl.num_programs(0) - 1)
    def _():
        pieces, kinds, rows, _ = own_grad_ref.shape
        for part, grad_ref in enumerate((own_grad_ref, other_grad_ref)):
            for kind in range(kinds):
                flipped = sums[kind, :, part * units : (part + 1) * units].astype(BF16).T
                for piece in range(pieces):
                    grad_ref[piece, kind] = flipped[piece * rows : (piece + 1) * rows]


def feed_forward(residual, cotangent, own, other, gain, pieces):
    tokens = residual.shape[0]
    tile = 256
    units = own.shape[1]
    spec = pl.BlockSpec((tile, D), lambda s: (s, 0))
    grad_shape = (pieces, 3, units // pieces, D)
    return pl.pallas_call(
        feed_body,
        grid=(tokens // tile,),
        in_specs=[
            spec,
            spec,
            whole(own.shape),
            whole(other.shape),
            whole(gain.shape),
        ],
        out_specs=[spec, spec, whole(grad_shape), whole(grad_shape), whole((1, D))],
        out_shape=[
            jax.ShapeDtypeStruct((tokens, D), BF16),
            jax.ShapeDtypeStruct((tokens, D), F32),
            jax.ShapeDtypeStruct(grad_shape, BF16),
            jax.ShapeDtypeStruct(grad_shape, BF16),
            jax.ShapeDtypeStruct((1, D), F32),
        ],
        scratch_shapes=[pltpu.VMEM((3, D, 2 * units), F32)],
        compiler_params=params(),
        cost_estimate=pl.CostEstimate(
            flops=32_000_000_000, transcendentals=6_000_000, bytes_accessed=30_000_000
        ),
        name="feed_forward",
    )(residual, cotangent, own, other, gain)


def attention_backward_body(
    x_ref,
    start_ref,
    weight_ref,
    gain_ref,
    cosine_ref,
    sine_ref,
    grad_ref,
    query_ref,
    key_ref,
    value_ref,
    mixed_ref,
    total_ref,
    tokens_ref,
    weight_grad_ref,
    gain_grad_ref,
    key_rows,
    value_rows,
    query_rows,
    grad_rows,
    grad_across,
    inner,
    grad_key,
    grad_value,
    grad_projected,
    sums,
):
    step = pl.program_id(0)
    length = x_ref.shape[1]
    cosine = cosine_ref[...]
    sine = sine_ref[...]

    @pl.when(step == 0)
    def _():
        sums[...] = jnp.zeros_like(sums)
        gain_grad_ref[...] = jnp.zeros_like(gain_grad_ref)

    branch = grad_ref[0].astype(BF16)
    sums[QKV:] += dot(mixed_ref[0], branch)
    grad_mixed = dot(weight_ref[QKV:], branch, 1, 1)
    for head in range(HEADS):
        rows = slice(head * 64, head * 64 + 64)
        part = grad_mixed[rows]
        grad_across[rows] = part.astype(BF16)
        grad_rows[head] = part.T.astype(BF16)
        query_rows[head] = query_ref[0, rows].T
        inner[head // RATIO, head % RATIO : head % RATIO + 1] = jnp.sum(
            part.astype(BF16).astype(F32) * mixed_ref[0, rows].astype(F32), axis=0, keepdims=True
        )
    for head in range(KV_HEADS):
        rows = slice(head * 64, head * 64 + 64)
        key_rows[head] = key_ref[0, rows].T
        value_rows[head] = value_ref[0, rows].T

    def group(member, carry):
        grad_key[...] = jnp.zeros_like(grad_key)
        grad_value[...] = jnp.zeros_like(grad_value)
        for block in range(length // BLOCK):
            low, high = block * BLOCK, (block + 1) * BLOCK
            heads = [member * 192 + r * 64 for r in range(RATIO)]
            queries = jnp.concatenate(
                [query_ref[0, pl.ds(h, 64), low:high] for h in heads], axis=1
            )
            grads = jnp.concatenate([grad_across[pl.ds(h, 64), low:high] for h in heads], axis=1)
            total = jnp.concatenate(
                [total_ref[0, member, r : r + 1, low:high] for r in range(RATIO)], axis=1
            )
            inner_row = jnp.concatenate(
                [inner[member, r : r + 1, low:high] for r in range(RATIO)], axis=1
            )
            start_row = triple(start_ref[0, 0:1, low:high])
            place_row = triple(lax.broadcasted_iota(jnp.int32, (1, BLOCK), 1) + low)
            scores = dot(key_rows[member, 0:high], queries)
            scores = visible_scores(scores, start_row, place_row, block)
            weights = jnp.exp(scores - total)
            grad_weights = dot(value_rows[member, 0:high], grads)
            grad_scores = (weights * (grad_weights - inner_row)).astype(BF16)
            grad_natural = jnp.concatenate(
                [grad_rows[member * RATIO + r, low:high] for r in range(RATIO)], axis=0
            )
            query_natural = jnp.concatenate(
                [query_rows[member * RATIO + r, low:high] for r in range(RATIO)], axis=0
            )
            grad_value[0:high] += dot(weights.astype(BF16), grad_natural)
            grad_key[0:high] += dot(grad_scores, query_natural)
            grad_query = dot(key_ref[0, pl.ds(member * 64, 64), 0:high], grad_scores)
            grad_query = grad_query * HEAD_DIM ** (-0.5)
            cos_part = triple(cosine[:, low:high])
            sin_part = triple(sine[:, low:high])
            front, behind = grad_query[:HALF], grad_query[HALF:]
            turned = jnp.concatenate(
                [front * cos_part + behind * sin_part, behind * cos_part - front * sin_part],
                axis=0,
            ).astype(BF16)
            for r in range(RATIO):
                grad_projected[pl.ds(heads[r], 64), low:high] = turned[
                    :, r * BLOCK : (r + 1) * BLOCK
                ]
        key_across = grad_key[...].T
        front, behind = key_across[:HALF], key_across[HALF:]
        grad_projected[pl.ds(D + member * 64, 64)] = jnp.concatenate(
            [front * cosine + behind * sine, behind * cosine - front * sine], axis=0
        ).astype(BF16)
        grad_projected[pl.ds(D + KV_WIDTH + member * 64, 64)] = grad_value[...].T.astype(BF16)
        return carry

    lax.fori_loop(0, KV_HEADS, group, 0)
    x = x_ref[0].astype(F32)
    gain = gain_ref[0:1]
    inverse = inverse_root(x)
    normal = x * inverse
    normed = (normal * gain).astype(BF16)
    projected = grad_projected[...]
    sums[:QKV] += dot(projected, normed)
    grad_normed = dot(projected.T, weight_ref[0:QKV])
    scaled = grad_normed * gain
    gain_grad_ref[...] += jnp.sum(grad_normed * normal, axis=0, keepdims=True)
    tokens_ref[0] = grad_ref[0] + inverse * (
        scaled - normal * jnp.mean(scaled * normal, axis=-1, keepdims=True)
    )

    @pl.when(step == pl.num_programs(0) - 1)
    def _():
        weight_grad_ref[...] = sums[...].astype(BF16)


def attention_backward(x, start, weights, gain, tables, grad, saved):
    count, length, _ = x.shape
    return pl.pallas_call(
        attention_backward_body,
        grid=(count,),
        in_specs=[
            row_block((length, D)),
            row_block((1, length)),
            whole(weights.shape),
            whole(gain.shape),
            whole((HALF, length)),
            whole((HALF, length)),
            row_block((length, D)),
        ]
        + [row_block(part.shape[1:]) for part in saved],
        out_specs=[row_block((length, D)), whole(weights.shape), whole((1, D))],
        out_shape=[
            jax.ShapeDtypeStruct((count, length, D), F32),
            jax.ShapeDtypeStruct(weights.shape, BF16),
            jax.ShapeDtypeStruct((1, D), F32),
        ],
        scratch_shapes=[
            pltpu.VMEM((KV_HEADS, length, HEAD_DIM), BF16),
            pltpu.VMEM((KV_HEADS, length, HEAD_DIM), BF16),
            pltpu.VMEM((HEADS, length, HEAD_DIM), BF16),
            pltpu.VMEM((HEADS, length, HEAD_DIM), BF16),
            pltpu.VMEM((D, length), BF16),
            pltpu.VMEM((KV_HEADS, 8, length), F32),
            pltpu.VMEM((length, HEAD_DIM), F32),
            pltpu.VMEM((length, HEAD_DIM), F32),
            pltpu.VMEM((QKV, length), BF16),
            pltpu.VMEM(weights.shape, F32),
        ],
        compiler_params=params(),
        cost_estimate=pl.CostEstimate(
            flops=17_000_000_000, transcendentals=12_000_000, bytes_accessed=25_000_000
        ),
        name="attention_backward",
    )(x, start, weights, gain, *tables, grad, *saved)


def factors(count):
    inner = 1 << ((count.bit_length() - 1) // 2)
    return count // inner, inner


def partner(values, mask):
    count = lax.axis_size("wide")
    return lax.ppermute(values, "wide", [(i, i ^ mask) for i in range(count)])


def across(values):
    return lax.ppermute(values, "narrow", [(0, 1), (1, 0)])


def in_order(parts, place):
    bit = 1
    while bit < len(parts):
        swap = (place & bit) != 0
        parts = [jnp.where(swap, parts[i ^ bit], part) for i, part in enumerate(parts)]
        bit *= 2
    return parts


def add_all(parts):
    total = parts[0].astype(F32)
    for part in parts[1:]:
        total = total + part.astype(F32)
    return total


def adamw_update(master, first_state, second_state, gradient, factor, step_rate, decay_rate):
    clipped = gradient * factor
    first_new = beta_first * first_state + (1.0 - beta_first) * clipped
    second_new = beta_second * second_state + (1.0 - beta_second) * clipped * clipped
    first_hat = first_new / (1.0 - beta_first**STEP)
    second_hat = second_new / (1.0 - beta_second**STEP)
    master_new = master * (1.0 - step_rate * decay_rate) - step_rate * first_hat / (
        jnp.sqrt(second_hat) + adam_epsilon
    )
    return (master_new, first_new, second_new)


def sum_everywhere(values):
    outer, inner = factors(lax.axis_size("wide"))
    values = values + across(values)
    values = add_all([values] + [partner(values, k) for k in range(1, inner)])
    return add_all([values] + [partner(values, k * inner) for k in range(1, outer)])


def per_device(
    tokens,
    cotangent,
    documents,
    attention_master,
    attention_first,
    attention_second,
    feedforward_master,
    feedforward_first,
    feedforward_second,
    gain_master,
    gain_first,
    gain_second,
):
    seq_count, half_len, _ = tokens.shape
    full_len = 2 * half_len
    own_count = seq_count // 2
    place = lax.axis_index("narrow")
    first = place == 0
    outer, inner = factors(lax.axis_size("wide"))
    wide_place = lax.axis_index("wide")
    outer_place, inner_place = wide_place // inner, wide_place % inner
    tables = rotary_tables(full_len)

    def keep_send(tensor):
        top, bottom = tensor[:own_count], tensor[own_count:]
        return jnp.where(first, top, bottom), jnp.where(first, bottom, top)

    def to_sequences(tensor):
        keep, send = keep_send(tensor)
        received = across(send)
        return jnp.concatenate(
            [jnp.where(first, keep, received), jnp.where(first, received, keep)], axis=1
        )

    def halves(tensor):
        left, right = tensor[:, :half_len], tensor[:, half_len:]
        return jnp.where(first, left, right), jnp.where(first, right, left)

    def to_positions(keep, received):
        return jnp.concatenate(
            [jnp.where(first, keep, received), jnp.where(first, received, keep)], axis=0
        )

    rows = attention_master.shape[0]
    piece = attention_master.astype(BF16)
    outer_parts = [piece] + [partner(piece, k * inner) for k in range(1, outer)]
    outer_stack = jnp.stack(in_order(outer_parts, outer_place))
    inner_parts = [outer_stack] + [partner(outer_stack, k) for k in range(1, inner)]
    inner_stack = jnp.stack(in_order(inner_parts, inner_place), axis=1)
    both = in_order([inner_stack, across(inner_stack)], place)
    attention_low = jnp.stack(both, axis=2).reshape(2 * inner * outer * rows, D)

    feed_piece = feedforward_master.astype(BF16)
    feed_outer = jnp.stack(
        [feed_piece] + [partner(feed_piece, k * inner) for k in range(1, outer)], axis=1
    )
    feed_own = jnp.stack(
        [feed_outer] + [partner(feed_outer, k) for k in range(1, inner)], axis=1
    ).reshape(3, -1, D)
    feed_other = across(feed_own)

    x = to_sequences(tokens)
    cotangent_rows = to_sequences(cotangent)
    own_docs = lax.dynamic_slice_in_dim(documents, place * own_count, own_count, 0)
    start = jnp.zeros_like(own_docs)
    for number in (1, 2):
        before = jnp.sum((own_docs < number).astype(jnp.int32), axis=1, keepdims=True)
        start = jnp.where(own_docs == number, before, start)
    start = start[:, None, :]

    residual, *saved = attention_forward(x, start, attention_low, gain_master, tables)
    flat = (own_count * full_len, D)
    out, back, own_grad, other_grad, gain_second_part = feed_forward(
        residual.reshape(flat), cotangent_rows.reshape(flat), feed_own, feed_other, gain_master, inner
    )
    keep, send = halves(out.reshape(own_count, full_len, D))
    outputs = to_positions(keep, across(send))

    received = across(other_grad)
    summed = [add_all([own_grad[k], received[k]]).astype(BF16) for k in range(inner)]
    summed = add_all([summed[0]] + [partner(summed[k], k) for k in range(1, inner)])
    summed = summed.reshape(3, outer, -1, D)
    feedforward_grad = add_all(
        [summed[:, 0]] + [partner(summed[:, k].astype(BF16), k * inner) for k in range(1, outer)]
    )

    grad_rows, weight_grad, gain_first_part = attention_backward(
        x, start, attention_low, gain_master, tables, back.reshape(own_count, full_len, D), saved
    )
    keep, send = halves(grad_rows)
    grad_tokens = to_positions(keep, across(send.astype(BF16)).astype(F32))

    weight_grad = weight_grad.reshape(outer, inner, 2, rows, D)
    even, odd = weight_grad[:, :, 0], weight_grad[:, :, 1]
    received = across(jnp.where(first, odd, even))
    summed = add_all([jnp.where(first, even, odd), received]).astype(BF16)
    parts = [
        lax.dynamic_index_in_dim(summed, inner_place ^ k, 1, keepdims=False) for k in range(inner)
    ]
    summed = add_all([parts[0]] + [partner(parts[k], k) for k in range(1, inner)])
    parts = [
        lax.dynamic_index_in_dim(summed, outer_place ^ k, 0, keepdims=False) for k in range(outer)
    ]
    attention_grad = add_all(
        [parts[0]] + [partner(parts[k].astype(BF16), k * inner) for k in range(1, outer)]
    )

    gain_grad = sum_everywhere(jnp.concatenate([gain_first_part, gain_second_part], axis=0))
    local_squares = jnp.sum(attention_grad * attention_grad) + jnp.sum(
        feedforward_grad * feedforward_grad
    )
    squares = sum_everywhere(jnp.full((1, 128), local_squares, F32))[0, 0]
    grad_norm = jnp.sqrt(squares + jnp.sum(gain_grad * gain_grad))
    factor = jnp.minimum(1.0, clip_limit / (grad_norm + 1e-06))
    update = functools.partial(adamw_update, factor=factor)
    attention_new = update(
        attention_master,
        attention_first,
        attention_second,
        attention_grad,
        step_rate=rate_matrix,
        decay_rate=weight_decay,
    )
    feedforward_new = update(
        feedforward_master,
        feedforward_first,
        feedforward_second,
        feedforward_grad,
        step_rate=rate_matrix,
        decay_rate=weight_decay,
    )
    gain_new = update(
        gain_master, gain_first, gain_second, gain_grad, step_rate=rate_gain, decay_rate=0.0
    )
    return (outputs, grad_tokens, grad_norm, *attention_new, *feedforward_new, *gain_new)


def solution(mesh):
    sequences = P("wide", "narrow", None)
    attention = P(("wide", "narrow"), None)
    feedforward = P(None, ("narrow", "wide"), None)
    state = (attention,) * 3 + (feedforward,) * 3 + (P(),) * 3
    return jax.shard_map(
        per_device,
        mesh=mesh,
        in_specs=(sequences, sequences, P("wide", None)) + state,
        out_specs=(sequences, sequences, P()) + state,
        check_vma=False,
    )
```

time: 1020 us -> 368 us (0.36)
  waiting for transfers between devices: 428 us -> 55 us
  matrix products: 339 us -> 0 us
  Pallas kernels: 0 us -> 141 us
  other arithmetic: 146 us -> 52.9 us
  starting transfers between devices: 1.13 us -> 50.8 us
  blocking collectives: 40.1 us -> 0 us
  between operations: 19.5 us -> 4.97 us
  local copies, waits for them, and re-layouts: 43.7 us -> 55.4 us
    dot_general x43 -> x0, matrix products: 339 us -> none  [the longest x4 53.5 us: attend_back(): jnp.einsum('gpkrd,glkd->gkrpl', grad_grouped, value_part, preferred_eleme...]
    unnamed x13 -> x0, waiting for transfers between devices: 223 us -> none
    pallas_call x0 -> x3, Pallas kernels: none -> 141 us  [the longest x1 56.8 us: feed_forward(): pl.pallas_call(feed_body, grid=(tokens // tile,), in_specs=[spec, spec, w...]
    reduce_scatter x5 -> x0, waiting for transfers between devices: 119 us -> none  [the longest x1 98.4 us: per_device(): lax.psum_scatter(jnp.concatenate([grad_qkv_rows, grad_out_rows], axis=0),...]
    all_gather x6 -> x0, waiting for transfers between devices: 86.2 us -> none  [the longest x1 57.9 us: per_device(): lax.all_gather(attention_master.astype(jnp.bfloat16), ('wide', 'narrow'),...]
    ppermute x0 -> x46, waiting for transfers between devices: none -> 55 us  [the longest x36 55 us: partner(): return lax.ppermute(values, 'wide', [(i, i ^ mask) for i in range(count)])]
    ppermute x0 -> x46, starting transfers between devices: none -> 50.8 us  [the longest x36 49.4 us: partner(): return lax.ppermute(values, 'wide', [(i, i ^ mask) for i in range(count)])]
    reduce_sum x7 -> x2, other arithmetic: 46.9 us -> 0.77 us  [the longest x1 0.61 us: per_device(): grad_norm = jnp.sqrt(squares + jnp.sum(gain_grad * gain_grad))]
  transfers between devices with their start and end apart: 12 -> 46, of which waited for: 8 -> 10; matrix products, arithmetic and copies ran while one was open for 22% -> 25% of each run, Pallas kernels for 0% -> 23%
where the time goes in v1:
time: 368 us; the launch traced here: 360 us
  Pallas kernels  141 us (38%)
  local copies, waits for them, and re-layouts  55.4 us (15%)
  waiting for transfers between devices  55 us (15%)
  other arithmetic  52.9 us (14%)
  starting transfers between devices  50.8 us (14%)
  between operations  4.97 us (1%)
    pallas_call x1, Pallas kernels, feed_forward(): pl.pallas_call(feed_body, grid=(tokens // tile,), in_specs=[spec, spec, w...  56.8 us
    ppermute x36, waiting for transfers between devices, partner(): return lax.ppermute(values, 'wide', [(i, i ^ mask) for i in range(count)])  55 us
    pallas_call x1, Pallas kernels, attention_backward(): pl.pallas_call(attention_backward_body, grid=(count,), in_specs=[row_bloc...  52.9 us
    ppermute x36, starting transfers between devices, partner(): return lax.ppermute(values, 'wide', [(i, i ^ mask) for i in range(count)])  49.4 us
    pallas_call x1, Pallas kernels, attention_forward(): pl.pallas_call(attention_forward_body, grid=(count,), in_specs=[row_block...  31.8 us
    unnamed x90, local copies, waits for them, and re-layouts  19.6 us
    ppermute x5, local copies, waits for them, and re-layouts, across(): return lax.ppermute(values, 'narrow', [(0, 1), (1, 0)])  15.2 us
  transfers between devices with their start and end apart: 46, of which 10 were waited for; matrix products, arithmetic and copies ran while one was open for 25% of the time, Pallas kernels for 23%

profile of v1, /device:TPU:0, one launch (start us, length us, event | category | flops | bytes accessed | tf_op | source)
XLA Modules:
  0.0 360.4 jit_solution(17354849675910189217)
XLA Ops:
  1.6 5.1 %collective-permute-start.1 = (bf16[48,576]{1,0:T(8,128)(2,1)S(1)}, bf16[48,576]{1,0:T(8,128)(2,1)S(1)}, u32[]{:S(2)}, u32[]{:S(2)}) collective-permute-start(bf16[48,576]{1,0:T(8,128)(2,1)S(1)} %convert_element_type.164), channel_id=1, source_target_pairs={{0,24},{2,26},{4,28},{6,30},{8,16},{10,18},{12,20},{14,22},{16,8},... | collective-permute-start | bytes 165896 | tf_op jit(solution)/shard_map/ppermute | solution.py:466
  7.3 1.7 convert_element_type.165
  9.0 1.4 collective-permute-start.9
  10.4 2.9 collective-permute-start.10
  13.3 2.9 fusion.30
  16.9 2.1 copy.89
  21.7 1.6 fusion.29
  26.2 2.4 collective-permute-start.4
  30.4 1.4 copy.65
  32.6 2.1 copy.91
  34.9 2.6 fusion.23
  37.5 1.5 collective-permute-start.12
  39.0 1.5 collective-permute-start.13
  41.0 1.3 select_bitcast_fusion.6
  42.3 1.4 select_bitcast_fusion.3
  46.9 2.4 copy.71
  49.3 7.8 %collective-permute-done.12 = bf16[3,4,48,576]{3,2,0,1:T(8,128)(2,1)} collective-permute-done((bf16[3,4,48,576]{3,2,0,1:T(8,128)(2,1)}, bf16[3,4,48,576]{3,2,0,1:T(8,128)(2,1)}, u32[]{:S(2)}, u32[]{:S(2)}) %collective-permute-start.12) | collective-permute-done | bytes 663584 | tf_op jit(solution)/shard_map/ppermute | solution.py:466
  57.1 16.2 %collective-permute-done.13 = bf16[3,4,48,576]{3,2,0,1:T(8,128)(2,1)} collective-permute-done((bf16[3,4,48,576]{3,2,0,1:T(8,128)(2,1)}, bf16[3,4,48,576]{3,2,0,1:T(8,128)(2,1)}, u32[]{:S(2)}, u32[]{:S(2)}) %collective-permute-start.13) | collective-permute-done | bytes 663584 | tf_op jit(solution)/shard_map/ppermute | solution.py:466
  73.3 1.9 pad_maximum_fusion.1
  75.6 3.5 copy.75
  79.9 1.7 select_bitcast_fusion.2
  81.9 1.5 copy.68
  83.4 2.5 copy.66
  85.9 2.5 copy.72
  88.4 1.6 broadcast_select_fusion.9
  90.0 1.8 pad_maximum_fusion.2.x_ref
  93.4 1.7 pad_maximum_fusion.3
  95.1 31.8 %attention_forward.1 = (f32[2,1024,576]{2,1,0:T(8,128)}, bf16[2,576,1024]{2,1,0:T(8,128)(2,1)}, bf16[2,192,1024]{2,1,0:T(8,128)(2,1)}, bf16[2,192,1024]{2,1,0:T(...) custom-call(bf16[2,1024,576]{2,1,0:T(8,128)(2,1)} %pad_maximum_fusion.2.x_ref, ...), custom_call_target="tpu_custom_call" | custom-call | flops 8000000000 | bytes 20000000 | tf_op jit(solution)/shard_map/attention_forward/pallas_call | solution.py:170
  126.9 5.4 %copy.76.other_ref = bf16[3,768,576]{2,1,0:T(8,128)(2,1)} copy(bf16[3,768,576]{1,2,0:T(8,128)(2,1)} %collective-permute-done.15) | data formatting | bytes 5308416 | tf_op jit(solution)/shard_map/ppermute | solution.py:470
  132.3 56.8 %feed_forward.1 = (bf16[2048,576]{1,0:T(8,128)(2,1)}, f32[2048,576]{1,0:T(8,128)}, bf16[4,3,192,576]{3,2,1,0:T(8,128)(2,1)}, bf16[4,3,192,576]{3,2,1,0:T(8,128)(2,1)}, f32[1,576]{1,0:T(1,128)}) custom-call(f32[2048,576]{1,0:T(8,128)} %bitcast.106, bf16[2048,576]{1,0:T(8,128)(2,1)} %bitcast.99, bf16[3,768,576]{2,1,0:T(8,128)(2,1)} %bitcast.94, ...), custom_call_target="tpu_custom_call" | custom-call | flops 32000000000 | bytes 30000000 | tf_op jit(solution)/shard_map/feed_forward/pallas_call | solution.py:265
  189.6 52.9 %attention_backward.1 = (f32[2,1024,576]{2,1,0:T(8,128)}, bf16[1536,576]{1,0:T(8,128)(2,1)}, f32[1,576]{1,0:T(1,128)}) custom-call(bf16[2,1024,576]{2,1,0:T(8,128)(2,1)} %pad_maximum_fusion.2.x_ref, s32[2,1,1024]{2,1,0:T(1,128)} %broadcast_in_dim.27.start_ref, bf16[1536,576]{1,0:T(8,128)(2,1)} %bitcast.101, f32[2,576]{1,0:T(2,128)} %gain_ref.5, ...), custom_call_target="tpu_custom_call" | custom-call | flops 16999999488 | bytes 25000000 | tf_op jit(solution)/shard_map/attention_backward/pallas_call | solution.py:420
  242.5 1.7 fusion.31
  245.9 2.8 select_convert_fusion
  248.6 1.4 copy.80
  252.2 1.4 collective-permute-start.42
  253.7 1.6 fusion
  255.3 1.3 collective-permute-start.19
  257.5 1.4 collective-permute-start.21
  258.9 5.4 %collective-permute-done.19 = bf16[4,48,576]{2,1,0:T(8,128)(2,1)S(1)} collective-permute-done((bf16[4,48,576]{2,1,0:T(8,128)(2,1)S(1)}, bf16[4,48,576]{2,1,0:T(8,128)(2,1)S(1)}, u32[]{:S(2)}, u32[]{:S(2)}) %collective-permute-start.19) | collective-permute-done | bytes 221216 | tf_op jit(solution)/shard_map/ppermute | solution.py:466
  264.3 3.2 collective-permute-done.20
  269.1 3.3 collective-permute-start.45
  272.7 3.4 fusion.4
  277.2 1.7 collective-permute-start.26
  278.9 1.5 collective-permute-start.27
  281.9 2.4 copy.77
  284.2 3.3 collective-permute-start.24
  288.1 2.2 collective-permute-done.24
  291.0 2.4 copy.81
  293.4 3.5 collective-permute-done.26
  296.9 13.0 %collective-permute-done.27 = bf16[3,192,576]{2,1,0:T(8,128)(2,1)} collective-permute-done((bf16[3,192,576]{2,1,0:T(8,128)(2,1)}, bf16[3,192,576]{2,1,0:T(8,128)(2,1)}, u32[]{:S(2)}, u32[]{:S(2)}) %collective-permute-start.27) | collective-permute-done | bytes 663584 | tf_op jit(solution)/shard_map/ppermute | solution.py:466
  309.9 2.5 fusion.2
  315.5 2.6 collective-permute-start.30
  318.7 5.4 %convert_select_fusion.1 = (f32[2,512,576]{2,1,0:T(8,128)}, f32[2,512,576]{2,1,0:T(8,128)}) fusion(bf16[2,512,576]{2,1,0:T(8,128)(2,1)S(1)} %copy-done.12, pred[]{:T(512)S(6)} %eq.11, f32[2,1024,576]{2,1,0:T(8,128)} %get-tuple-element.34), kind=kLoop, calls=%fused_computation.2 | loop fusion | flops 2359296 | bytes 10616833 | tf_op jit(solution)/shard_map/jit(_where)/select_n | solution.py:549
  324.0 2.4 copy.78
  326.5 2.4 collective-permute-done.30
  328.9 1.8 multiply_reduce_fusion
  332.1 1.8 broadcast_select_fusion.1
  336.1 1.4 collective-permute-start.35
  337.5 2.7 pad_maximum_fusion
  340.6 2.6 collective-permute-start.36
  344.2 1.4 collective-permute-start.38
  346.0 5.7 %copy.87 = f32[4,512,576]{1,2,0:T(8,128)} copy(f32[4,512,576]{2,1,0:T(8,128)} %pad_maximum_fusion) | data formatting | bytes 9437184
  351.7 2.5 copy.86
  355.8 2.3 divide_subtract_fusion
  (184 shorter events, 37.3 us)
Async XLA Ops:
  1.6 21.7 %collective-permute-start.1 = (bf16[48,576]{1,0:T(8,128)(2,1)S(1)}, bf16[48,576]{1,0:T(8,128)(2,1)S(1)}, u32[]{:S(2)}, u32[]{:S(2)}) collective-permute-start(bf16[48,576]{1,0:T(8,128)(2,1)S(1)} %convert_element_type.164), channel_id=1, source_target_pairs={{0,24},{2,26},{4,28},{6,30},{8,16},{10,18},{12,20},{14,22},{16,8},... | collective-permute-start | bytes 165896 | tf_op jit(solution)/shard_map/ppermute | solution.py:466
  6.7 16.7 %collective-permute-start.2 = (bf16[48,576]{1,0:T(8,128)(2,1)S(1)}, bf16[48,576]{1,0:T(8,128)(2,1)S(1)}, u32[]{:S(2)}, u32[]{:S(2)}) collective-permute-start(bf16[48,576]{1,0:T(8,128)(2,1)S(1)} %convert_element_type.164), channel_id=1, source_target_pairs={{0,16},{2,18},{4,20},{6,22},{8,24},{10,26},{12,28},{14,30},{16,0},... | collective-permute-start | bytes 165896 | tf_op jit(solution)/shard_map/ppermute | solution.py:466
  6.7 17.8 %collective-permute-start.3 = (bf16[48,576]{1,0:T(8,128)(2,1)S(1)}, bf16[48,576]{1,0:T(8,128)(2,1)}, u32[]{:S(2)}, u32[]{:S(2)}) collective-permute-start(bf16[48,576]{1,0:T(8,128)(2,1)S(1)} %convert_element_type.164), channel_id=1, source_target_pairs={{0,8},{2,10},{4,12},{6,14},{8,0},{10,2},{12,4},{14,6},{16,24},{18,... | collective-permute-start | bytes 165896 | tf_op jit(solution)/shard_map/ppermute | solution.py:466
  9.0 20.2 %collective-permute-start.9 = (bf16[3,48,576]{2,1,0:T(8,128)(2,1)}, bf16[3,48,576]{2,1,0:T(8,128)(2,1)S(1)}, u32[]{:S(2)}, u32[]{:S(2)}) collective-permute-start(bf16[3,48,576]{2,1,0:T(8,128)(2,1)} %convert_element_type.165), channel_id=1, source_target_pairs={{0,8},{2,10},{4,12},{6,14},{8,0},{10,2},{12,4},{14,6},{16,24},{18,... | collective-permute-start | bytes 497672 | tf_op jit(solution)/shard_map/ppermute | solution.py:466
  10.4 24.4 %collective-permute-start.10 = (bf16[3,48,576]{2,1,0:T(8,128)(2,1)}, bf16[3,48,576]{2,1,0:T(8,128)(2,1)}, u32[]{:S(2)}, u32[]{:S(2)}) collective-permute-start(bf16[3,48,576]{2,1,0:T(8,128)(2,1)} %convert_element_type.165), channel_id=1, source_target_pairs={{0,16},{2,18},{4,20},{6,22},{8,24},{10,26},{12,28},{14,30},{16,0},... | collective-permute-start | bytes 497672 | tf_op jit(solution)/shard_map/ppermute | solution.py:466
  21.7 8.0 %copy-start.17 = (f32[3,48,576]{2,1,0:T(8,128)S(1)}, f32[3,48,576]{2,1,0:T(8,128)}, u32[]{:S(2)}) copy-start(f32[3,48,576]{2,1,0:T(8,128)} %param.20) | copy-start | bytes 995332
  23.2 7.2 %copy-start.13 = (bf16[2,512,576]{2,1,0:T(8,128)(2,1)S(1)}, bf16[2,512,576]{2,1,0:T(8,128)(2,1)}, u32[]{:S(2)}) copy-start(bf16[2,512,576]{2,1,0:T(8,128)(2,1)} %broadcast_select_fusion.10) | copy-start | bytes 3538948
  23.3 11.6 %collective-permute-start.11 = (bf16[3,48,576]{2,1,0:T(8,128)(2,1)}, bf16[3,48,576]{2,1,0:T(8,128)(2,1)}, u32[]{:S(2)}, u32[]{:S(2)}) collective-permute-start(bf16[3,48,576]{2,1,0:T(8,128)(2,1)} %convert_element_type.165), channel_id=1, source_target_pairs={{0,24},{2,26},{4,28},{6,30},{8,16},{10,18},{12,20},{14,22},{16,8},... | collective-permute-start | bytes 497672 | tf_op jit(solution)/shard_map/ppermute | solution.py:466
  25.4 6.4 %copy-start.29 = (bf16[1,48,576]{2,1,0:T(8,128)(2,1)}, bf16[1,48,576]{2,1,0:T(8,128)(2,1)S(1)}, u32[]{:S(2)}) copy-start(bf16[1,48,576]{2,1,0:T(8,128)(2,1)S(1)} %get-tuple-element.129) | copy-start | bytes 165892
  26.2 5.7 %copy-start.15 = (bf16[2,512,576]{1,2,0:T(8,128)(2,1)S(1)}, bf16[2,512,576]{1,2,0:T(8,128)(2,1)}, u32[]{:S(2)}) copy-start(bf16[2,512,576]{1,2,0:T(8,128)(2,1)} %get-tuple-element.104) | copy-start | bytes 3538948
  26.2 12.8 %collective-permute-start.4 = (bf16[4,48,576]{2,1,0:T(8,128)(2,1)}, bf16[4,48,576]{2,1,0:T(8,128)(2,1)}, u32[]{:S(2)}, u32[]{:S(2)}) collective-permute-start(bf16[4,48,576]{2,1,0:T(8,128)(2,1)} %pad_maximum_fusion.8), channel_id=1, source_target_pairs={{0,6},{2,4},{4,2},{6,0},{8,14},{10,12},{12,10},{14,8},{16,22},{18,... | collective-permute-start | bytes 663560 | tf_op jit(solution)/shard_map/ppermute | solution.py:466
  28.7 11.8 %collective-permute-start.5 = (bf16[4,48,576]{2,1,0:T(8,128)(2,1)}, bf16[4,48,576]{2,1,0:T(8,128)(2,1)}, u32[]{:S(2)}, u32[]{:S(2)}) collective-permute-start(bf16[4,48,576]{2,1,0:T(8,128)(2,1)} %pad_maximum_fusion.8), channel_id=1, source_target_pairs={{0,4},{2,6},{4,0},{6,2},{8,12},{10,14},{12,8},{14,10},{16,20},{18,... | collective-permute-start | bytes 663560 | tf_op jit(solution)/shard_map/ppermute | solution.py:466
  29.2 11.8 %collective-permute-start.6 = (bf16[4,48,576]{2,1,0:T(8,128)(2,1)}, bf16[4,48,576]{2,1,0:T(8,128)(2,1)}, u32[]{:S(2)}, u32[]{:S(2)}) collective-permute-start(bf16[4,48,576]{2,1,0:T(8,128)(2,1)} %pad_maximum_fusion.8), channel_id=1, source_target_pairs={{0,2},{2,0},{4,6},{6,4},{8,10},{10,8},{12,14},{14,12},{16,18},{18,... | collective-permute-start | bytes 663560 | tf_op jit(solution)/shard_map/ppermute | solution.py:466
  32.6 13.1 %copy-start.5 = (bf16[2,512,576]{2,1,0:T(8,128)(2,1)}, bf16[2,512,576]{2,1,0:T(8,128)(2,1)S(1)}, u32[]{:S(2)}) copy-start(bf16[2,512,576]{2,1,0:T(8,128)(2,1)S(1)} %copy.90) | copy-start | bytes 3538948
  34.7 11.0 %copy-start.7 = (bf16[2,512,576]{2,1,0:T(8,128)(2,1)}, bf16[2,512,576]{2,1,0:T(8,128)(2,1)S(1)}, u32[]{:S(2)}) copy-start(bf16[2,512,576]{2,1,0:T(8,128)(2,1)S(1)} %copy.91) | copy-start | bytes 3538948
  34.8 6.2 %copy-start.30 = (bf16[1,48,576]{2,1,0:T(8,128)(2,1)S(1)}, bf16[1,48,576]{2,1,0:T(8,128)(2,1)}, u32[]{:S(2)}) copy-start(bf16[1,48,576]{2,1,0:T(8,128)(2,1)} %copy-done.29) | copy-start | bytes 165892
  34.8 48.6 %collective-permute-start = (bf16[2,512,576]{1,2,0:T(8,128)(2,1)}, bf16[2,512,576]{1,2,0:T(8,128)(2,1)}, u32[]{:S(2)}, u32[]{:S(2)}) collective-permute-start(bf16[2,512,576]{1,2,0:T(8,128)(2,1)} %copy.65), channel_id=1, source_target_pairs={{0,1},{1,0},{2,3},{3,2},{4,5},{5,4},{6,7},{7,6},{8,9},{9,8},{10,11... | collective-permute-start | bytes 3538952 | tf_op jit(solution)/shard_map/ppermute | solution.py:470
  37.5 19.7 %collective-permute-start.12 = (bf16[3,4,48,576]{3,2,0,1:T(8,128)(2,1)}, bf16[3,4,48,576]{3,2,0,1:T(8,128)(2,1)}, u32[]{:S(2)}, u32[]{:S(2)}) collective-permute-start(bf16[3,4,48,576]{3,2,0,1:T(8,128)(2,1)} %get-tuple-element.122), channel_id=1, source_target_pairs={{0,2},{2,0},{4,6},{6,4},{8,10},{10,8},{12,14},{14,12},{16,18},{18,... | collective-permute-start | bytes 1990664 | tf_op jit(solution)/shard_map/ppermute | solution.py:466
  39.0 34.3 %collective-permute-start.13 = (bf16[3,4,48,576]{3,2,0,1:T(8,128)(2,1)}, bf16[3,4,48,576]{3,2,0,1:T(8,128)(2,1)}, u32[]{:S(2)}, u32[]{:S(2)}) collective-permute-start(bf16[3,4,48,576]{3,2,0,1:T(8,128)(2,1)} %get-tuple-element.122), channel_id=1, source_target_pairs={{0,4},{2,6},{4,0},{6,2},{8,12},{10,14},{12,8},{14,10},{16,20},{18,... | collective-permute-start | bytes 1990664 | tf_op jit(solution)/shard_map/ppermute | solution.py:466
  40.5 32.8 %collective-permute-start.14 = (bf16[3,4,48,576]{3,2,0,1:T(8,128)(2,1)}, bf16[3,4,48,576]{3,2,0,1:T(8,128)(2,1)}, u32[]{:S(2)}, u32[]{:S(2)}) collective-permute-start(bf16[3,4,48,576]{3,2,0,1:T(8,128)(2,1)} %get-tuple-element.122), channel_id=1, source_target_pairs={{0,6},{2,4},{4,2},{6,0},{8,14},{10,12},{12,10},{14,8},{16,22},{18,... | collective-permute-start | bytes 1990664 | tf_op jit(solution)/shard_map/ppermute | solution.py:466
  45.6 34.3 %collective-permute-start.7 = (bf16[4,4,48,576]{3,2,0,1:T(8,128)(2,1)}, bf16[4,4,48,576]{3,2,0,1:T(8,128)(2,1)}, u32[]{:S(2)}, u32[]{:S(2)}) collective-permute-start(bf16[4,4,48,576]{3,2,0,1:T(8,128)(2,1)} %pad_maximum_fusion.6), channel_id=1, source_target_pairs={{0,1},{1,0},{2,3},{3,2},{4,5},{5,4},{6,7},{7,6},{8,9},{9,8},{10,11... | collective-permute-start | bytes 2654216 | tf_op jit(solution)/shard_map/ppermute | solution.py:470
  57.1 28.8 %collective-permute-start.8 = (bf16[2,512,576]{1,2,0:T(8,128)(2,1)}, bf16[2,512,576]{1,2,0:T(8,128)(2,1)}, u32[]{:S(2)}, u32[]{:S(2)}) collective-permute-start(bf16[2,512,576]{1,2,0:T(8,128)(2,1)} %copy.71), channel_id=1, source_target_pairs={{0,1},{1,0},{2,3},{3,2},{4,5},{5,4},{6,7},{7,6},{8,9},{9,8},{10,11... | collective-permute-start | bytes 3538952 | tf_op jit(solution)/shard_map/ppermute | solution.py:470
  75.6 4.3 %copy-start.22 = (bf16[4,1,48,576]{3,2,0,1:T(8,128)(2,1)S(1)}, bf16[4,1,48,576]{3,2,0,1:T(8,128)(2,1)}, u32[]{:S(2)}) copy-start(bf16[4,1,48,576]{3,2,0,1:T(8,128)(2,1)} %copy-done.21) | copy-start | bytes 663556
  75.6 4.3 %copy-start.24 = (bf16[4,1,48,576]{3,2,0,1:T(8,128)(2,1)S(1)}, bf16[4,1,48,576]{3,2,0,1:T(8,128)(2,1)}, u32[]{:S(2)}) copy-start(bf16[4,1,48,576]{3,2,0,1:T(8,128)(2,1)} %copy-done.23) | copy-start | bytes 663556
  79.0 47.8 %collective-permute-start.15 = (bf16[3,768,576]{1,2,0:T(8,128)(2,1)}, bf16[3,768,576]{1,2,0:T(8,128)(2,1)}, u32[]{:S(2)}, u32[]{:S(2)}) collective-permute-start(bf16[3,768,576]{1,2,0:T(8,128)(2,1)} %copy.75), channel_id=1, source_target_pairs={{0,1},{1,0},{2,3},{3,2},{4,5},{5,4},{6,7},{7,6},{8,9},{9,8},{10,11... | collective-permute-start | bytes 7962632 | tf_op jit(solution)/shard_map/ppermute | solution.py:470
  83.4 5.0 %copy-start.4 = (bf16[2,512,576]{2,1,0:T(8,128)(2,1)S(1)}, bf16[2,512,576]{2,1,0:T(8,128)(2,1)}, u32[]{:S(2)}) copy-start(bf16[2,512,576]{2,1,0:T(8,128)(2,1)} %copy-done.3) | copy-start | bytes 3538948
  189.0 83.5 %collective-permute-start.25 = (bf16[4,3,192,576]{3,2,1,0:T(8,128)(2,1)}, bf16[4,3,192,576]{3,2,1,0:T(8,128)(2,1)}, u32[]{:S(2)}, u32[]{:S(2)}) collective-permute-start(bf16[4,3,192,576]{3,2,1,0:T(8,128)(2,1)} %get-tuple-element.37), channel_id=1, source_target_pairs={{0,1},{1,0},{2,3},{3,2},{4,5},{5,4},{6,7},{7,6},{8,9},{9,8},{10,11... | collective-permute-start | bytes 7962632 | tf_op jit(solution)/shard_map/ppermute | solution.py:470
  245.3 7.0 %collective-permute-start.18 = (bf16[4,4,48,576]{3,2,0,1:T(8,128)(2,1)}, bf16[4,4,48,576]{3,2,0,1:T(8,128)(2,1)}, u32[]{:S(2)}, u32[]{:S(2)}) collective-permute-start(bf16[4,4,48,576]{3,2,0,1:T(8,128)(2,1)} %select_bitcast_fusion), channel_id=1, source_target_pairs={{0,1},{1,0},{2,3},{3,2},{4,5},{5,4},{6,7},{7,6},{8,9},{9,8},{10,11... | collective-permute-start | bytes 2654216 | tf_op jit(solution)/shard_map/ppermute | solution.py:470
  245.3 4.8 %collective-permute-start.39 = (f32[2,576]{1,0:T(2,128)S(1)}, f32[2,576]{1,0:T(2,128)S(1)}, u32[]{:S(2)}, u32[]{:S(2)}) collective-permute-start(f32[2,576]{1,0:T(2,128)S(1)} %pad_maximum_fusion.9), channel_id=1, source_target_pairs={{0,1},{1,0},{2,3},{3,2},{4,5},{5,4},{6,7},{7,6},{8,9},{9,8},{10,11... | collective-permute-start | bytes 13832 | tf_op jit(solution)/shard_map/ppermute | solution.py:470
  250.1 40.9 %collective-permute-start.17 = (bf16[2,512,576]{1,2,0:T(8,128)(2,1)}, bf16[2,512,576]{1,2,0:T(8,128)(2,1)}, u32[]{:S(2)}, u32[]{:S(2)}) collective-permute-start(bf16[2,512,576]{1,2,0:T(8,128)(2,1)} %copy.80), channel_id=1, source_target_pairs={{0,1},{1,0},{2,3},{3,2},{4,5},{5,4},{6,7},{7,6},{8,9},{9,8},{10,11... | collective-permute-start | bytes 3538952 | tf_op jit(solution)/shard_map/ppermute | solution.py:470
  250.1 5.2 %collective-permute-start.40 = (f32[2,576]{1,0:T(2,128)S(1)}, f32[2,576]{1,0:T(2,128)S(1)}, u32[]{:S(2)}, u32[]{:S(2)}) collective-permute-start(f32[2,576]{1,0:T(2,128)S(1)} %fusion.22), channel_id=1, source_target_pairs={{0,2},{2,0},{4,6},{6,4},{8,10},{10,8},{12,14},{14,12},{16,18},{18,... | collective-permute-start | bytes 13832 | tf_op jit(solution)/shard_map/ppermute | solution.py:466
  251.4 5.2 %collective-permute-start.41 = (f32[2,576]{1,0:T(2,128)S(1)}, f32[2,576]{1,0:T(2,128)S(1)}, u32[]{:S(2)}, u32[]{:S(2)}) collective-permute-start(f32[2,576]{1,0:T(2,128)S(1)} %fusion.22), channel_id=1, source_target_pairs={{0,4},{2,6},{4,0},{6,2},{8,12},{10,14},{12,8},{14,10},{16,20},{18,... | collective-permute-start | bytes 13832 | tf_op jit(solution)/shard_map/ppermute | solution.py:466
  252.2 5.2 %collective-permute-start.42 = (f32[2,576]{1,0:T(2,128)S(1)}, f32[2,576]{1,0:T(2,128)S(1)}, u32[]{:S(2)}, u32[]{:S(2)}) collective-permute-start(f32[2,576]{1,0:T(2,128)S(1)} %fusion.22), channel_id=1, source_target_pairs={{0,6},{2,4},{4,2},{6,0},{8,14},{10,12},{12,10},{14,8},{16,22},{18,... | collective-permute-start | bytes 13832 | tf_op jit(solution)/shard_map/ppermute | solution.py:466
  255.2 17.4 %copy-start.19 = (bf16[4,3,192,576]{3,2,1,0:T(8,128)(2,1)S(1)}, bf16[4,3,192,576]{3,2,1,0:T(8,128)(2,1)}, u32[]{:S(2)}) copy-start(bf16[4,3,192,576]{3,2,1,0:T(8,128)(2,1)} %get-tuple-element.36) | copy-start | bytes 7962628
  255.3 8.9 %collective-permute-start.19 = (bf16[4,48,576]{2,1,0:T(8,128)(2,1)S(1)}, bf16[4,48,576]{2,1,0:T(8,128)(2,1)S(1)}, u32[]{:S(2)}, u32[]{:S(2)}) collective-permute-start(bf16[4,48,576]{2,1,0:T(8,128)(2,1)S(1)} %get-tuple-element.112), channel_id=1, source_target_pairs={{0,2},{2,0},{4,6},{6,4},{8,10},{10,8},{12,14},{14,12},{16,18},{18,... | collective-permute-start | bytes 663560 | tf_op jit(solution)/shard_map/ppermute | solution.py:466
  256.6 10.9 %collective-permute-start.20 = (bf16[4,48,576]{2,1,0:T(8,128)(2,1)S(1)}, bf16[4,48,576]{2,1,0:T(8,128)(2,1)S(1)}, u32[]{:S(2)}, u32[]{:S(2)}) collective-permute-start(bf16[4,48,576]{2,1,0:T(8,128)(2,1)S(1)} %get-tuple-element.114), channel_id=1, source_target_pairs={{0,4},{2,6},{4,0},{6,2},{8,12},{10,14},{12,8},{14,10},{16,20},{18,... | collective-permute-start | bytes 663560 | tf_op jit(solution)/shard_map/ppermute | solution.py:466
  257.5 11.7 %collective-permute-start.21 = (bf16[4,48,576]{2,1,0:T(8,128)(2,1)S(1)}, bf16[4,48,576]{2,1,0:T(8,128)(2,1)S(1)}, u32[]{:S(2)}, u32[]{:S(2)}) collective-permute-start(bf16[4,48,576]{2,1,0:T(8,128)(2,1)S(1)} %get-tuple-element.113), channel_id=1, source_target_pairs={{0,6},{2,4},{4,2},{6,0},{8,14},{10,12},{12,10},{14,8},{16,22},{18,... | collective-permute-start | bytes 663560 | tf_op jit(solution)/shard_map/ppermute | solution.py:466
  264.3 11.8 %collective-permute-start.43 = (f32[2,576]{1,0:T(2,128)S(1)}, f32[2,576]{1,0:T(2,128)S(1)}, u32[]{:S(2)}, u32[]{:S(2)}) collective-permute-start(f32[2,576]{1,0:T(2,128)S(1)} %add_add_fusion.1), channel_id=1, source_target_pairs={{0,8},{2,10},{4,12},{6,14},{8,0},{10,2},{12,4},{14,6},{16,24},{18,... | collective-permute-start | bytes 13832 | tf_op jit(solution)/shard_map/ppermute | solution.py:466
  267.5 9.7 %collective-permute-start.44 = (f32[2,576]{1,0:T(2,128)S(1)}, f32[2,576]{1,0:T(2,128)S(1)}, u32[]{:S(2)}, u32[]{:S(2)}) collective-permute-start(f32[2,576]{1,0:T(2,128)S(1)} %add_add_fusion.1), channel_id=1, source_target_pairs={{0,16},{2,18},{4,20},{6,22},{8,24},{10,26},{12,28},{14,30},{16,0},... | collective-permute-start | bytes 13832 | tf_op jit(solution)/shard_map/ppermute | solution.py:466
  269.1 9.8 %collective-permute-start.45 = (f32[2,576]{1,0:T(2,128)S(1)}, f32[2,576]{1,0:T(2,128)S(1)}, u32[]{:S(2)}, u32[]{:S(2)}) collective-permute-start(f32[2,576]{1,0:T(2,128)S(1)} %add_add_fusion.1), channel_id=1, source_target_pairs={{0,24},{2,26},{4,28},{6,30},{8,16},{10,18},{12,20},{14,22},{16,8},... | collective-permute-start | bytes 13832 | tf_op jit(solution)/shard_map/ppermute | solution.py:466
  272.6 7.9 %collective-permute-start.22 = (bf16[48,576]{1,0:T(8,128)(2,1)S(1)}, bf16[48,576]{1,0:T(8,128)(2,1)S(1)}, u32[]{:S(2)}, u32[]{:S(2)}) collective-permute-start(bf16[48,576]{1,0:T(8,128)(2,1)S(1)} %get-tuple-element.123), channel_id=1, source_target_pairs={{0,8},{2,10},{4,12},{6,14},{8,0},{10,2},{12,4},{14,6},{16,24},{18,... | collective-permute-start | bytes 165896 | tf_op jit(solution)/shard_map/ppermute | solution.py:466
  272.7 8.0 %copy-start.9 = (bf16[2048,576]{1,0:T(8,128)(2,1)S(1)}, bf16[2048,576]{1,0:T(8,128)(2,1)}, u32[]{:S(2)}) copy-start(bf16[2048,576]{1,0:T(8,128)(2,1)} %get-tuple-element.27) | copy-start | bytes 7077892
  276.1 8.2 %collective-permute-start.23 = (bf16[48,576]{1,0:T(8,128)(2,1)S(1)}, bf16[48,576]{1,0:T(8,128)(2,1)S(1)}, u32[]{:S(2)}, u32[]{:S(2)}) collective-permute-start(bf16[48,576]{1,0:T(8,128)(2,1)S(1)} %get-tuple-element.125), channel_id=1, source_target_pairs={{0,16},{2,18},{4,20},{6,22},{8,24},{10,26},{12,28},{14,30},{16,0},... | collective-permute-start | bytes 165896 | tf_op jit(solution)/shard_map/ppermute | solution.py:466
  277.2 19.7 %collective-permute-start.26 = (bf16[3,192,576]{2,1,0:T(8,128)(2,1)}, bf16[3,192,576]{2,1,0:T(8,128)(2,1)}, u32[]{:S(2)}, u32[]{:S(2)}) collective-permute-start(bf16[3,192,576]{2,1,0:T(8,128)(2,1)} %get-tuple-element.95), channel_id=1, source_target_pairs={{0,2},{2,0},{4,6},{6,4},{8,10},{10,8},{12,14},{14,12},{16,18},{18,... | collective-permute-start | bytes 1990664 | tf_op jit(solution)/shard_map/ppermute | solution.py:466
  278.9 31.0 %collective-permute-start.27 = (bf16[3,192,576]{2,1,0:T(8,128)(2,1)}, bf16[3,192,576]{2,1,0:T(8,128)(2,1)}, u32[]{:S(2)}, u32[]{:S(2)}) collective-permute-start(bf16[3,192,576]{2,1,0:T(8,128)(2,1)} %get-tuple-element.97), channel_id=1, source_target_pairs={{0,4},{2,6},{4,0},{6,2},{8,12},{10,14},{12,8},{14,10},{16,20},{18,... | collective-permute-start | bytes 1990664 | tf_op jit(solution)/shard_map/ppermute | solution.py:466
  280.4 29.5 %collective-permute-start.28 = (bf16[3,192,576]{2,1,0:T(8,128)(2,1)}, bf16[3,192,576]{2,1,0:T(8,128)(2,1)}, u32[]{:S(2)}, u32[]{:S(2)}) collective-permute-start(bf16[3,192,576]{2,1,0:T(8,128)(2,1)} %get-tuple-element.96), channel_id=1, source_target_pairs={{0,6},{2,4},{4,2},{6,0},{8,14},{10,12},{12,10},{14,8},{16,22},{18,... | collective-permute-start | bytes 1990664 | tf_op jit(solution)/shard_map/ppermute | solution.py:466
  284.2 6.1 %collective-permute-start.24 = (bf16[48,576]{1,0:T(8,128)(2,1)S(1)}, bf16[48,576]{1,0:T(8,128)(2,1)S(1)}, u32[]{:S(2)}, u32[]{:S(2)}) collective-permute-start(bf16[48,576]{1,0:T(8,128)(2,1)S(1)} %get-tuple-element.124), channel_id=1, source_target_pairs={{0,24},{2,26},{4,28},{6,30},{8,16},{10,18},{12,20},{14,22},{16,8},... | collective-permute-start | bytes 165896 | tf_op jit(solution)/shard_map/ppermute | solution.py:466
  290.4 33.7 %collective-permute-start.16 = (bf16[2,512,576]{1,2,0:T(8,128)(2,1)}, bf16[2,512,576]{1,2,0:T(8,128)(2,1)}, u32[]{:S(2)}, u32[]{:S(2)}) collective-permute-start(bf16[2,512,576]{1,2,0:T(8,128)(2,1)} %copy.77), channel_id=1, source_target_pairs={{0,1},{1,0},{2,3},{3,2},{4,5},{5,4},{6,7},{7,6},{8,9},{9,8},{10,11... | collective-permute-start | bytes 3538952 | tf_op jit(solution)/shard_map/ppermute | solution.py:470
  309.9 8.8 %copy-start.12 = (bf16[2,512,576]{2,1,0:T(8,128)(2,1)S(1)}, bf16[2,512,576]{2,1,0:T(8,128)(2,1)}, u32[]{:S(2)}) copy-start(bf16[2,512,576]{2,1,0:T(8,128)(2,1)} %copy.81) | copy-start | bytes 3538948
  314.3 12.2 %collective-permute-start.29 = (bf16[3,48,576]{2,1,0:T(8,128)(2,1)}, bf16[3,48,576]{2,1,0:T(8,128)(2,1)S(1)}, u32[]{:S(2)}, u32[]{:S(2)}) collective-permute-start(bf16[3,48,576]{2,1,0:T(8,128)(2,1)} %get-tuple-element.118), channel_id=1, source_target_pairs={{0,8},{2,10},{4,12},{6,14},{8,0},{10,2},{12,4},{14,6},{16,24},{18,... | collective-permute-start | bytes 497672 | tf_op jit(solution)/shard_map/ppermute | solution.py:466
  315.5 13.4 %collective-permute-start.30 = (bf16[3,48,576]{2,1,0:T(8,128)(2,1)S(1)}, bf16[3,48,576]{2,1,0:T(8,128)(2,1)S(1)}, u32[]{:S(2)}, u32[]{:S(2)}) collective-permute-start(bf16[3,48,576]{2,1,0:T(8,128)(2,1)S(1)} %get-tuple-element.120), channel_id=1, source_target_pairs={{0,16},{2,18},{4,20},{6,22},{8,24},{10,26},{12,28},{14,30},{16,0},... | collective-permute-start | bytes 497672 | tf_op jit(solution)/shard_map/ppermute | solution.py:466
  318.1 10.8 %collective-permute-start.31 = (bf16[3,48,576]{2,1,0:T(8,128)(2,1)S(1)}, bf16[3,48,576]{2,1,0:T(8,128)(2,1)}, u32[]{:S(2)}, u32[]{:S(2)}) collective-permute-start(bf16[3,48,576]{2,1,0:T(8,128)(2,1)S(1)} %get-tuple-element.119), channel_id=1, source_target_pairs={{0,24},{2,26},{4,28},{6,30},{8,16},{10,18},{12,20},{14,22},{16,8},... | collective-permute-start | bytes 497672 | tf_op jit(solution)/shard_map/ppermute | solution.py:466
  332.0 1.9 collective-permute-start.32
  332.1 5.4 %copy-start.10 = (f32[2,512,576]{2,1,0:T(8,128)S(1)}, f32[2,512,576]{2,1,0:T(8,128)}, u32[]{:S(2)}) copy-start(f32[2,512,576]{2,1,0:T(8,128)} %get-tuple-element.93) | copy-start | bytes 7077892
  332.1 5.4 %copy-start.11 = (f32[2,512,576]{2,1,0:T(8,128)S(1)}, f32[2,512,576]{2,1,0:T(8,128)}, u32[]{:S(2)}) copy-start(f32[2,512,576]{2,1,0:T(8,128)} %get-tuple-element.94) | copy-start | bytes 7077892
  333.9 6.2 %collective-permute-start.33 = (f32[1,128]{1,0:T(1,128)S(1)}, f32[1,128]{1,0:T(1,128)S(1)}, u32[]{:S(2)}, u32[]{:S(2)}) collective-permute-start(f32[1,128]{1,0:T(1,128)S(1)} %broadcast_add_fusion), channel_id=1, source_target_pairs={{0,2},{2,0},{4,6},{6,4},{8,10},{10,8},{12,14},{14,12},{16,18},{18,... | collective-permute-start | bytes 1544 | tf_op jit(solution)/shard_map/ppermute | solution.py:466
  335.0 5.2 %collective-permute-start.34 = (f32[1,128]{1,0:T(1,128)S(1)}, f32[1,128]{1,0:T(1,128)S(1)}, u32[]{:S(2)}, u32[]{:S(2)}) collective-permute-start(f32[1,128]{1,0:T(1,128)S(1)} %broadcast_add_fusion), channel_id=1, source_target_pairs={{0,4},{2,6},{4,0},{6,2},{8,12},{10,14},{12,8},{14,10},{16,20},{18,... | collective-permute-start | bytes 1544 | tf_op jit(solution)/shard_map/ppermute | solution.py:466
  336.1 4.4 %collective-permute-start.35 = (f32[1,128]{1,0:T(1,128)S(1)}, f32[1,128]{1,0:T(1,128)S(1)}, u32[]{:S(2)}, u32[]{:S(2)}) collective-permute-start(f32[1,128]{1,0:T(1,128)S(1)} %broadcast_add_fusion), channel_id=1, source_target_pairs={{0,6},{2,4},{4,2},{6,0},{8,14},{10,12},{12,10},{14,8},{16,22},{18,... | collective-permute-start | bytes 1544 | tf_op jit(solution)/shard_map/ppermute | solution.py:466
  340.6 13.7 %collective-permute-start.36 = (f32[1,128]{1,0:T(1,128)S(1)}, f32[1,128]{1,0:T(1,128)S(1)}, u32[]{:S(2)}, u32[]{:S(2)}) collective-permute-start(f32[1,128]{1,0:T(1,128)S(1)} %add_add_fusion.3), channel_id=1, source_target_pairs={{0,8},{2,10},{4,12},{6,14},{8,0},{10,2},{12,4},{14,6},{16,24},{18,... | collective-permute-start | bytes 1544 | tf_op jit(solution)/shard_map/ppermute | solution.py:466
  343.2 11.1 %collective-permute-start.37 = (f32[1,128]{1,0:T(1,128)S(1)}, f32[1,128]{1,0:T(1,128)S(1)}, u32[]{:S(2)}, u32[]{:S(2)}) collective-permute-start(f32[1,128]{1,0:T(1,128)S(1)} %add_add_fusion.3), channel_id=1, source_target_pairs={{0,16},{2,18},{4,20},{6,22},{8,24},{10,26},{12,28},{14,30},{16,0},... | collective-permute-start | bytes 1544 | tf_op jit(solution)/shard_map/ppermute | solution.py:466
  344.2 10.0 %collective-permute-start.38 = (f32[1,128]{1,0:T(1,128)S(1)}, f32[1,128]{1,0:T(1,128)S(1)}, u32[]{:S(2)}, u32[]{:S(2)}) collective-permute-start(f32[1,128]{1,0:T(1,128)S(1)} %add_add_fusion.3), channel_id=1, source_target_pairs={{0,24},{2,26},{4,28},{6,30},{8,16},{10,18},{12,20},{14,22},{16,8},... | collective-permute-start | bytes 1544 | tf_op jit(solution)/shard_map/ppermute | solution.py:466
  351.7 4.1 %copy-start.18 = (f32[3,48,576]{2,1,0:T(8,128)S(1)}, f32[3,48,576]{2,1,0:T(8,128)}, u32[]{:S(2)}) copy-start(f32[3,48,576]{2,1,0:T(8,128)} %param.20) | copy-start | bytes 995332
  354.2 3.8 %copy-start.32 = (f32[48,576]{1,0:T(8,128)S(1)}, f32[48,576]{1,0:T(8,128)}, u32[]{:S(2)}) copy-start(f32[48,576]{1,0:T(8,128)} %param.18) | copy-start | bytes 331780
  354.2 3.8 %copy-start.33 = (f32[48,576]{1,0:T(8,128)S(1)}, f32[48,576]{1,0:T(8,128)}, u32[]{:S(2)}) copy-start(f32[48,576]{1,0:T(8,128)} %param.19) | copy-start | bytes 331780
  (24 other events, 59.4 us)
